TPU v7x, 32 devices: a whole 2x2x4 slice. The times are simulated.
32 devices in a mesh: fsdp: 4 (over y, x), ctx: 4 (over z), tp: 2 (over core).
Axes of the slice: x: 2, y: 2, z: 4, core: 2. Of those that a mesh axis runs over, the one named last changes fastest.
Arguments:
- image_input: bfloat16 [4, 2048, 768], P('fsdp', 'ctx'), may hold values from -6 to 6
- image_segments: int32 [4, 2048], P('fsdp'), may hold values from 0 to 5, never falling along the last dimension, each value on 1 to 1536 neighbouring positions
- image_cotangent: bfloat16 [4, 2048, 768], P('fsdp', 'ctx'), may hold values from -6 to 6
- image_gains: bfloat16 [2, 768], P(None, 'fsdp'), may hold values from 0.099609375 to 1.8984375
- image_shifts: bfloat16 [4, 768], P(None, 'fsdp'), may hold values from -3 to 3
- image_head_bias: bfloat16 [2, 2304], P('tp', 'fsdp'), may hold values from -3 to 3
- image_qkv_weight: bfloat16 [3, 768, 768], P(None, 'fsdp', 'tp'), may hold values from -0.21875 to 0.21875
- image_proj_weight: bfloat16 [768, 768], P('tp', 'fsdp'), may hold values from -0.875 to 0.875
- image_up_weight: bfloat16 [768, 3072], P('fsdp', 'tp'), may hold values from -0.21875 to 0.21875
- image_down_weight: bfloat16 [3072, 768], P('tp', 'fsdp'), may hold values from -0.109375 to 0.109375
- text_input: bfloat16 [4, 2048, 512], P('fsdp', 'ctx'), may hold values from -6 to 6
- text_segments: int32 [4, 2048], P('fsdp'), may hold values from 0 to 5, never falling along the last dimension, each value on 1 to 1536 neighbouring positions
- text_cotangent: bfloat16 [4, 2048, 512], P('fsdp', 'ctx'), may hold values from -6 to 6
- text_gains: bfloat16 [2, 512], P(None, 'fsdp'), may hold values from 0.099609375 to 1.8984375
- text_shifts: bfloat16 [4, 512], P(None, 'fsdp'), may hold values from -3 to 3
- text_head_bias: bfloat16 [2, 1536], P('tp', 'fsdp'), may hold values from -3 to 3
- text_qkv_weight: bfloat16 [3, 512, 512], P(None, 'fsdp', 'tp'), may hold values from -0.25 to 0.25
- text_proj_weight: bfloat16 [512, 512], P('tp', 'fsdp'), may hold values from -1 to 1
- text_up_weight: bfloat16 [512, 2048], P('fsdp', 'tp'), may hold values from -0.25 to 0.25
- text_down_weight: bfloat16 [2048, 512], P('tp', 'fsdp'), may hold values from -0.125 to 0.125
Outputs:
- image_output: bfloat16 [4, 2048, 768], P('fsdp', 'ctx')
- image_input_grad: float32 [4, 2048, 768], P('fsdp', 'ctx')
- image_gains_grad: float32 [2, 768], P(None, 'fsdp')
- image_shifts_grad: float32 [4, 768], P(None, 'fsdp')
- image_head_bias_grad: float32 [2, 2304], P('tp', 'fsdp')
- image_qkv_grad: float32 [3, 768, 768], P(None, 'fsdp', 'tp')
- image_proj_grad: float32 [768, 768], P('tp', 'fsdp')
- image_up_grad: float32 [768, 3072], P('fsdp', 'tp')
- image_down_grad: float32 [3072, 768], P('tp', 'fsdp')
- text_output: bfloat16 [4, 2048, 512], P('fsdp', 'ctx')
- text_input_grad: float32 [4, 2048, 512], P('fsdp', 'ctx')
- text_gains_grad: float32 [2, 512], P(None, 'fsdp')
- text_shifts_grad: float32 [4, 512], P(None, 'fsdp')
- text_head_bias_grad: float32 [2, 1536], P('tp', 'fsdp')
- text_qkv_grad: float32 [3, 512, 512], P(None, 'fsdp', 'tp')
- text_proj_grad: float32 [512, 512], P('tp', 'fsdp')
- text_up_grad: float32 [512, 2048], P('fsdp', 'tp')
- text_down_grad: float32 [2048, 512], P('tp', 'fsdp')
Inputs may be any that keep to these rules, and one draw needn't show every extreme that they name: `image_segments`: along each sequence segment numbers never fall; every document has 1 to 1536 tokens, and one has exactly that many. `text_segments`: along each sequence segment numbers never fall; every document has 1 to 1536 tokens, and one has exactly that many.
All inputs are finite; a program needn't handle non-finite values.
Results may differ from a plain program's by a relative error of at most 0.012.
Values may be sent and summed in bfloat16 or wider, within the bound.
A program may use at most 128 MiB of HBM per device.

v0:
```python
import functools

import jax
import jax.numpy as jnp
from jax import lax
from jax.experimental import pallas as pl
from jax.experimental.pallas import tpu as pltpu
from jax.sharding import PartitionSpec as P

HD = 64
LANES = 128
QB = 256
KB = 512
NEG = -1e30
F32 = jnp.float32
MESH = pl.DeviceIdType.MESH
FSDP, CTX, TP = "fsdp", "ctx", "tp"
BF16 = jnp.bfloat16


def dot(left, right, dims=((1,), (0,))):
    return lax.dot_general(left, right, (dims, ((), ())), preferred_element_type=F32)


def lane_marks():
    lane = lax.broadcasted_iota(jnp.int32, (1, LANES), 1)
    first = (lane < HD).astype(F32).astype(BF16)
    second = (lane >= HD).astype(F32).astype(BF16)
    return first, second


def document_columns(row_ref, out_ref):
    for start in range(0, out_ref.shape[0], LANES):
        row = row_ref[:, start : start + LANES].astype(F32)
        out_ref[start : start + LANES, :] = jnp.transpose(jnp.broadcast_to(row, (LANES, LANES)))


def swap_halves(value):
    return pltpu.roll(value, HD, 1)


def key_range(index):
    return slice(index * KB, (index + 1) * KB)


def mix_rows(query, seg_query, keys, seg_keys, own, other, diagonal=None):
    query = query * own
    scores = []
    for block, seg in zip(keys, seg_keys):
        score = dot(query, block, ((1,), (1,)))
        ok = seg_query == seg.astype(F32)
        if diagonal is not None and len(scores) == len(keys) - 1:
            key_pos = lax.broadcasted_iota(jnp.int32, score.shape, 1)
            query_pos = diagonal + lax.broadcasted_iota(jnp.int32, score.shape, 0)
            ok = jnp.logical_and(ok, key_pos <= query_pos)
        scores.append(jnp.where(ok, score, NEG))
    top = jnp.max(functools.reduce(jnp.maximum, scores), axis=1, keepdims=True)
    acc = jnp.zeros((query.shape[0], LANES), F32)
    for score, block in zip(scores, keys):
        acc = acc + dot(jnp.exp(score - top).astype(BF16), block * other + own)
    return acc / swap_halves(acc), top + jnp.log(acc)


def pick(flag, one, zero):
    return jnp.where(flag == 1, one, zero)


def attend_text(m, seg_col, seg_row, o, lse):
    first, second = lane_marks()
    lane = lax.broadcasted_iota(jnp.int32, (QB, LANES), 1)
    o[...] = jnp.zeros_like(o)
    for source in range(4):
        keys = [m[i, QB:] for i in range(source + 1)]
        segs = [seg_row[:, key_range(i)] for i in range(source + 1)]

        def one(half, carry, source=source, keys=keys, segs=segs):
            query = m[source, :QB].astype(F32)
            query = pick(half, swap_halves(query), query).astype(BF16)
            tokens = pl.ds(pl.multiple_of(source * KB + half * QB, QB), QB)
            mixed, log_total = mix_rows(
                query, seg_col[tokens, :1], keys, segs, first, second, half * QB
            )
            lse[2 * source + half, :8] = jnp.transpose(log_total)[:8]
            mixed = pick(half, mixed, swap_halves(mixed))
            o[source] = jnp.where(lane // HD == half, mixed.astype(BF16), o[source])
            return carry

        lax.fori_loop(0, 2, one, 0)


def image_task(at, task):
    extra = 1 - (task + 8) // 12
    block = pick(extra, at.here_low * 4 + task, task - 4)
    source, half = block // 2, block % 2
    rows = pl.ds(pl.multiple_of(half * QB, QB), QB)
    tokens = pl.ds(pl.multiple_of(block * QB, QB), QB)
    return extra, block, source, rows, tokens


def task_marks(extra):
    first, second = lane_marks()
    return pick(extra, second, first), pick(extra, first, second)


def attend_image(at, m, seg_col, seg_row, o, lse):
    lane = lax.broadcasted_iota(jnp.int32, (QB, LANES), 1)
    segs = [seg_row[:, key_range(i)] for i in range(4)]
    o[...] = jnp.zeros_like(o)

    def one(task, carry):
        extra, block, source, rows, tokens = image_task(at, task)
        own, other = task_marks(extra)
        mixed, log_total = mix_rows(
            m[source, 0, rows],
            seg_col[tokens, :1],
            [m[i, 1 + extra] for i in range(4)],
            segs,
            own,
            other,
        )
        log_total = jnp.transpose(log_total)
        lse[block, pl.ds(pl.multiple_of(8 * extra, 8), 8)] = pick(
            extra, log_total[HD : HD + 8], log_total[:8]
        )
        o[source, rows] = jnp.where(lane // HD == 1 - extra, mixed.astype(BF16), o[source, rows])
        return carry

    lax.fori_loop(0, 12, one, 0)


def unmix_rows(query, grad_o, seg_query, keys, seg_keys, totals, lse, delta, own, other, diagonal=None):
    query, grad_o = query * own, grad_o * other
    grad_query = jnp.zeros((query.shape[0], LANES), F32)
    for index, (block, seg, (total, rows)) in enumerate(zip(keys, seg_keys, totals)):
        score = dot(block, query, ((1,), (1,)))
        ok = seg == seg_query
        if diagonal is not None and index == len(keys) - 1:
            key_pos = lax.broadcasted_iota(jnp.int32, score.shape, 0)
            query_pos = diagonal + lax.broadcasted_iota(jnp.int32, score.shape, 1)
            ok = jnp.logical_and(ok, key_pos <= query_pos)
        weights = jnp.where(ok, jnp.exp(score - lse), 0.0)
        grad_weights = dot(block, grad_o, ((1,), (1,)))
        grad_scores = (weights * (grad_weights - delta)).astype(BF16)
        total[rows, :] += dot(grad_scores, query) + dot(weights.astype(BF16), grad_o)
        grad_query = grad_query + dot(grad_scores, block, ((0,), (0,)))
    return grad_query * 0.125


def unattend_text(m, do, o, lse, seg_col, seg_row, acc, out):
    first, second = lane_marks()
    lane = lax.broadcasted_iota(jnp.int32, (QB, LANES), 1)
    acc[...] = jnp.zeros_like(acc)
    out[:, :QB] = jnp.zeros((4, QB, LANES), BF16)
    for source in range(4):
        keys = [m[i, QB:] for i in range(source + 1)]
        segs = [seg_col[key_range(i), :1] for i in range(source + 1)]
        totals = [(acc, key_range(i)) for i in range(source + 1)]

        def one(half, carry, source=source, keys=keys, segs=segs, totals=totals):
            query, grad_o = m[source, :QB].astype(F32), do[source].astype(F32)
            product = jnp.transpose(grad_o * o[source].astype(F32))
            query = pick(half, swap_halves(query), query).astype(BF16)
            grad_o = pick(half, grad_o, swap_halves(grad_o)).astype(BF16)
            tokens = pl.ds(pl.multiple_of(source * KB + half * QB, QB), QB)
            grad_query = unmix_rows(
                query,
                grad_o,
                seg_row[:, tokens].astype(F32),
                keys,
                segs,
                totals,
                lse[2 * source + half, :1],
                jnp.sum(pick(half, product[HD:], product[:HD]), axis=0, keepdims=True),
                first,
                second,
                half * QB,
            )
            grad_query = pick(half, swap_halves(grad_query), grad_query).astype(BF16)
            out[source, :QB] = jnp.where(lane // HD == half, grad_query, out[source, :QB])
            return carry

        lax.fori_loop(0, 2, one, 0)
    for source in range(4):
        out[source, QB:] = acc[key_range(source)].astype(BF16)


def unattend_image(at, m, do, o, lse, seg_col, seg_row, acc, out, begin, end):
    lane = lax.broadcasted_iota(jnp.int32, (QB, LANES), 1)
    segs = [seg_col[key_range(i), :1] for i in range(4)]

    def one(task, carry):
        extra, block, source, rows, tokens = image_task(at, task)
        own, other = task_marks(extra)
        grad_o = do[source, rows]
        product = jnp.transpose(grad_o.astype(F32) * o[source, rows].astype(F32))
        grad_query = unmix_rows(
            m[source, 0, rows],
            grad_o,
            seg_row[:, tokens].astype(F32),
            [m[i, 1 + extra] for i in range(4)],
            segs,
            [(acc.at[extra], key_range(i)) for i in range(4)],
            lse[block, pl.ds(pl.multiple_of(8 * extra, 8), 8)][:1],
            jnp.sum(pick(extra, product[:HD], product[HD:]), axis=0, keepdims=True),
            own,
            other,
        ).astype(BF16)
        out[source, 0, rows] = jnp.where(lane // HD == extra, grad_query, out[source, 0, rows])
        return carry

    lax.fori_loop(begin, end, one, 0)


class Bag:
    pass


def partners():
    at = Bag()
    group, here, core = lax.axis_index(FSDP), lax.axis_index(CTX), lax.axis_index(TP)
    at.group, at.here = group, here
    at.group_x = group + 1 - 2 * (group % 2)
    at.group_y = group + 2 - 4 * (group // 2)
    at.group_far = 3 - group
    at.here_low, at.here_high = here % 2, here // 2
    at.inner, at.outer = (here + 1) // 2 == 1, (here + 1) // 2 != 1
    at.ctx = (here, here + 1 - 2 * (here % 2), here + 2 - 4 * (here // 2), 3 - here)
    at.to_x, at.to_y, at.to_far = ({FSDP: g} for g in (at.group_x, at.group_y, at.group_far))
    at.to_ctx = [{CTX: c} for c in at.ctx]
    at.to_core = {TP: 1 - core}
    return at


def meet(devices):
    barrier = pltpu.get_barrier_semaphore()
    for device in devices:
        pl.semaphore_signal(barrier, inc=1, device_id=device, device_id_type=MESH)
    pl.semaphore_wait(barrier, len(devices))


class Copies:
    def __init__(self, send_sems, recv_sems, local_sems):
        self.sems = (send_sems, recv_sems, local_sems)
        self.used = [0, 0]

    def remote(self, src, dst, device, start=True):
        index = self.used[0]
        self.used[0] += 1
        copy = pltpu.make_async_remote_copy(
            src_ref=src,
            dst_ref=dst,
            send_sem=self.sems[0].at[index],
            recv_sem=self.sems[1].at[index],
            device_id=device,
            device_id_type=MESH,
        )
        if start:
            copy.start()
        return copy

    def local(self, src, dst):
        index = self.used[1]
        self.used[1] += 1
        copy = pltpu.make_async_copy(src, dst, self.sems[2].at[index])
        copy.start()
        return copy


def copy_sems(remote, local):
    return [
        pltpu.SemaphoreType.DMA((remote,)),
        pltpu.SemaphoreType.DMA((remote,)),
        pltpu.SemaphoreType.DMA((local,)),
    ]


class Gather:
    def __init__(self, copies, at, src, dst):
        self.copies, self.at, self.dst = copies, at, dst
        self.rows = src.shape[-2]
        own = self.part(at.group, 0, self.rows)
        self.own = copies.local(src, own)
        self.to_x = copies.remote(src, own, at.to_x)
        self.to_y = copies.remote(src, own, at.to_y)

    def part(self, owner, offset, size):
        rows = pl.ds(pl.multiple_of(owner * self.rows + offset, 8), size)
        return self.dst.at[:, rows, :] if len(self.dst.shape) == 3 else self.dst.at[rows, :]

    def forward(self):
        half = self.rows // 2
        self.to_x.wait_recv()
        self.to_y.wait_recv()
        top = self.part(self.at.group_y, 0, half)
        low = self.part(self.at.group_x, half, half)
        self.far_x = self.copies.remote(top, top, self.at.to_x)
        self.far_y = self.copies.remote(low, low, self.at.to_y)

    def arrived(self):
        self.own.wait()
        self.far_x.wait_recv()
        self.far_y.wait_recv()

    def sent(self):
        for copy in (self.to_x, self.to_y, self.far_x, self.far_y):
            copy.wait_send()


def normalise(rows):
    mean = jnp.mean(rows, axis=-1, keepdims=True)
    centred = rows - mean
    inv = lax.rsqrt(jnp.mean(centred * centred, axis=-1, keepdims=True) + 1e-05)
    return centred * inv, inv


def lane_pair(low, high):
    lane = lax.broadcasted_iota(jnp.int32, low[0].shape, 1)
    left = low[0] if low[1] == 0 else pltpu.roll(low[0], HD, 1)
    right = high[0] if high[1] == 1 else pltpu.roll(high[0], HD, 1)
    return jnp.where(lane < HD, left, right)


def head_tile(ref, start, index, rows=slice(None)):
    first = start + (index // 2) * LANES
    return ref[rows, first : first + LANES], index % 2


def write_messages(qkv, out, heads):
    width = heads * HD
    tokens = qkv.shape[0]
    for c in range(4):
        if heads == 4:
            half = tokens // 2
            out[c, :half] = lane_pair(
                head_tile(qkv, 0, c, slice(0, half)), head_tile(qkv, 0, c, slice(half, None))
            ).astype(BF16)
            out[c, half:] = lane_pair(
                head_tile(qkv, width, c), head_tile(qkv, 2 * width, c)
            ).astype(BF16)
        else:
            e = 4 + c // 2
            out[c, 0] = lane_pair(head_tile(qkv, 0, c), head_tile(qkv, 0, e)).astype(BF16)
            out[c, 1] = lane_pair(
                head_tile(qkv, width, c), head_tile(qkv, 2 * width, c)
            ).astype(BF16)
            out[c, 2] = lane_pair(
                head_tile(qkv, 2 * width, e), head_tile(qkv, width, e)
            ).astype(BF16)


def message_shape(heads, tokens):
    part = (tokens // 2 + tokens, LANES) if heads == 4 else (3, tokens, LANES)
    return (4,) + part


def first_rows(x_ref, small_ref, weight_ref, first_ref, qkv_ref, step):
    width = weight_ref.shape[2]
    rows = slice(step * 256, step * 256 + 256)
    normed, _ = normalise(x_ref[rows, :].astype(F32))
    first = (normed * small_ref[0:1] + small_ref[2:3]).astype(BF16)
    first_ref[:, rows] = jnp.transpose(first)
    bias = small_ref[6:7]
    qkv_ref[rows, :width] = (dot(first, weight_ref[0]) + bias[:, :width]) * 0.125
    qkv_ref[rows, width : 2 * width] = dot(first, weight_ref[1])
    qkv_ref[rows, 2 * width :] = dot(first, weight_ref[2]) + bias[:, width : 2 * width]


def spread_small(at, gains, shifts, bias, wide, flat, out):
    width = wide.shape[1]
    columns, bias_columns = gains.shape[1], bias.shape[1]
    wide[...] = jnp.zeros_like(wide)
    flat[...] = jnp.zeros_like(flat)
    wide[0:2, :columns] = gains[...].astype(F32)
    wide[2:6, :columns] = shifts[...].astype(F32)
    flat[0:1, :bias_columns] = bias[...].astype(F32)
    out[0:8] = pltpu.roll(wide[...], at.group * columns, 1)
    line = pltpu.roll(flat[...], at.group * bias_columns, 1)
    out[8:16] = jnp.zeros((8, width), F32)
    for row in range(3):
        out[6 + row : 7 + row] = line[0:1, row * width : (row + 1) * width]


FRONT_IN, FRONT_OUT, FRONT_SCRATCH = 9, 10, 10


def front_kernel(*refs):
    at = partners()
    ins = [refs[:FRONT_IN], refs[FRONT_IN : 2 * FRONT_IN]]
    refs = refs[2 * FRONT_IN :]
    outs = [refs[:FRONT_OUT], refs[FRONT_OUT : 2 * FRONT_OUT]]
    refs = refs[2 * FRONT_OUT :]
    scratch = [refs[:FRONT_SCRATCH], refs[FRONT_SCRATCH : 2 * FRONT_SCRATCH]]
    copies = Copies(*refs[2 * FRONT_SCRATCH :])
    streams = []
    for in_refs, out_refs, own in zip(ins, outs, scratch):
        s = Bag()
        s.x, s.seg_row, s.gains, s.shifts, s.bias, s.qkv, s.up, s.down, s.proj = in_refs
        (
            s.weight, s.small, s.first, s.messages, s.proj_full, s.up_full, s.down_full, s.o, s.lse,
            s.o_got,
        ) = out_refs
        (
            s.small_in, s.small_own, s.wide, s.flat, s.rows, s.mine, s.got, s.down_t, s.proj_t, s.seg_col,
        ) = own
        s.heads = s.weight.shape[2] // HD
        streams.append(s)
    meet([at.to_x, at.to_y, at.to_far] + at.to_ctx[1:])
    text, image = streams
    image.gather = Gather(copies, at, image.qkv, image.weight)
    for s in (image, text):
        spread_small(at, s.gains, s.shifts, s.bias, s.wide, s.flat, s.small_own)
    for s in (image, text):
        s.small_done = [
            copies.remote(s.small_own, s.small_in.at[i], device)
            for i, device in enumerate((at.to_x, at.to_y, at.to_far))
        ]
    image.gather.forward()
    text.gather = Gather(copies, at, text.qkv, text.weight)
    text.down_t[...] = jnp.transpose(text.down[...])
    text.proj_t[...] = jnp.transpose(text.proj[...])
    for s in (image, text):
        document_columns(s.seg_row, s.seg_col)

    def project(s):
        for copy in s.small_done:
            copy.wait_recv()
        s.small[...] = s.small_own[...] + s.small_in[0] + s.small_in[1] + s.small_in[2]
        s.gather.arrived()
        for step in range(s.x.shape[0] // 256):
            first_rows(s.x, s.small, s.weight, s.first, s.rows, step)
        write_messages(s.rows, s.mine, s.heads)
        s.sends = send_blocks(copies, at, s.mine, s.got)

    def gather_rest(s):
        pieces = (s.proj_t, s.up, s.down_t) if s.heads == 4 else (s.proj, s.up, s.down)
        s.rest = [
            Gather(copies, at, piece, full)
            for piece, full in zip(pieces, (s.proj_full, s.up_full, s.down_full))
        ]

    project(image)
    text.gather.forward()
    gather_rest(image)
    project(text)
    gather_rest(text)
    for gather in image.rest:
        gather.forward()
    for copy in image.sends:
        copy.wait()
    image.keep = copies.local(image.got, image.messages)
    attend_image(at, image.got, image.seg_col, image.seg_row, image.o, image.lse)
    image.o_done = send_blocks(copies, at, image.o, image.o_got)
    for gather in text.rest:
        gather.forward()
    for copy in text.sends:
        copy.wait()
    text.keep = copies.local(text.got, text.messages)
    attend_text(text.got, text.seg_col, text.seg_row, text.o, text.lse)
    text.o_done = send_blocks(copies, at, text.o, text.o_got)
    for s in (image, text):
        for gather in s.rest:
            gather.arrived()
        for gather in [s.gather] + s.rest:
            gather.sent()
        for copy in s.small_done:
            copy.wait_send()
        s.keep.wait()
        for copy in s.o_done:
            copy.wait()


def front(streams):
    vmem, hbm = pl.BlockSpec(memory_space=pltpu.VMEM), pl.BlockSpec(memory_space=pl.ANY)
    out_shape, out_specs, scratch = [], [], []
    for x, seg, gains, shifts, bias, qkv, up, down, proj in streams:
        tokens, width = x.shape
        own = qkv.shape[2]
        messages = message_shape(own // HD, tokens)
        hidden = up.shape[1]
        small = jax.ShapeDtypeStruct((16, width), F32)
        out_shape += [
            jax.ShapeDtypeStruct((3, width, own), BF16),
            small,
            jax.ShapeDtypeStruct((width, tokens), BF16),
            jax.ShapeDtypeStruct(messages, BF16),
            jax.ShapeDtypeStruct((width, own), BF16),
            jax.ShapeDtypeStruct((width, hidden), BF16),
            jax.ShapeDtypeStruct((width, hidden), BF16),
            jax.ShapeDtypeStruct((4, QB if own == 4 * HD else KB, LANES), BF16),
            jax.ShapeDtypeStruct((4 * tokens // QB, 16, QB), F32),
            jax.ShapeDtypeStruct((4, QB if own == 4 * HD else KB, LANES), BF16),
        ]
        out_specs += [vmem, vmem, vmem, hbm, hbm, hbm, hbm, vmem, vmem, hbm]
        scratch += [
            pltpu.VMEM((3, 16, width), F32),
            pltpu.VMEM((16, width), F32),
            pltpu.VMEM((8, width), F32),
            pltpu.VMEM((8, 3 * width), F32),
            pltpu.VMEM((tokens, 3 * own), F32),
            pltpu.VMEM(messages, BF16),
            pltpu.VMEM(messages, BF16),
            pltpu.VMEM((width // 4, hidden), BF16),
            pltpu.VMEM((width // 4, own), BF16),
            pltpu.VMEM((4 * tokens, LANES), F32),
        ]
    results = pl.pallas_call(
        front_kernel,
        out_shape=out_shape,
        in_specs=[vmem] * (2 * FRONT_IN),
        out_specs=out_specs,
        scratch_shapes=scratch + copy_sems(2 * (3 + 4 * 4 + 6), 2 * 7),
        compiler_params=pltpu.CompilerParams(
            collective_id=0, has_side_effects=True, vmem_limit_bytes=63 << 20
        ),
        name="front",
    )(*streams[0], *streams[1])
    return results[:FRONT_OUT], results[FRONT_OUT:]


STEP = 384


def by_columns(columns, body):
    def one(index, carry):
        body(pl.ds(pl.multiple_of(index * STEP, STEP), STEP))
        return carry

    lax.fori_loop(0, columns // STEP, one, 0)


class PlaneSum:
    def __init__(self, copies, at, src, arrivals, loads=None):
        self.copies, self.at = copies, at
        self.in_x, self.in_y, self.in_top, self.in_low = arrivals
        half, self.columns = self.in_top.shape
        self.half, rows = half, 2 * half

        def block(owner, offset, size=half):
            return src.at[pl.ds(pl.multiple_of(owner * rows + offset, 8), size), :]

        self.first = [
            copies.remote(block(at.group_far, 0), self.in_x.at[1], at.to_x),
            copies.remote(block(at.group_far, half), self.in_y.at[1], at.to_y),
            copies.remote(block(at.group_x, 0), self.in_x.at[0], at.to_x),
            copies.remote(block(at.group_y, half), self.in_y.at[0], at.to_y),
        ]
        parts = [block(at.group_y, 0), block(at.group_x, half), block(at.group, 0, rows)]
        if loads is None:
            self.loads = []
            self.pass_top, self.pass_low, self.own = parts
        else:
            self.loads = [copies.local(part, load) for part, load in zip(parts, loads)]
            self.pass_top, self.pass_low, self.own = loads

    def cross(self):
        for copy in self.loads:
            copy.wait()
        self.first[0].wait_recv()

        def top(cols):
            self.pass_top[:, cols] = (
                self.pass_top[:, cols].astype(F32) + self.in_x[1, :, cols].astype(F32)
            ).astype(BF16)

        by_columns(self.columns, top)
        self.second = [self.copies.remote(self.pass_top, self.in_top, self.at.to_y)]
        self.first[1].wait_recv()

        def low(cols):
            self.pass_low[:, cols] = (
                self.pass_low[:, cols].astype(F32) + self.in_y[1, :, cols].astype(F32)
            ).astype(BF16)

        by_columns(self.columns, low)
        self.second.append(self.copies.remote(self.pass_low, self.in_low, self.at.to_x))

    def arrived(self):
        for copy in self.first[2:] + self.second:
            copy.wait_recv()

    def halves(self, cols):
        half = self.half
        return (
            self.own[:half, cols].astype(F32)
            + self.in_x[0, :, cols].astype(F32)
            + self.in_top[:, cols].astype(F32),
            self.own[half:, cols].astype(F32)
            + self.in_y[0, :, cols].astype(F32)
            + self.in_low[:, cols].astype(F32),
        )

    def sent(self):
        for copy in self.first + self.second:
            copy.wait_send()

    @staticmethod
    def arrivals(rows, columns):
        half = rows // 2
        pair, one = pltpu.VMEM((2, half, columns), BF16), pltpu.VMEM((half, columns), BF16)
        return [pair, pair, one, one]

    @staticmethod
    def loads_scratch(rows, columns):
        half = rows // 2
        one = pltpu.VMEM((half, columns), BF16)
        return [one, one, pltpu.VMEM((rows, columns), BF16)]


class LineSum:
    def __init__(self, copies, at, values, buffers, final, begin, end):
        self.at, self.values, self.final, self.range = at, values, final, (begin, end)
        self.pair, self.outer_in, self.inner_in = buffers

        def part(ref):
            return ref.at[:, begin:end]

        self.up = copies.remote(part(self.pair), part(self.outer_in), at.to_ctx[1], False)
        self.across = copies.remote(part(self.pair), part(self.inner_in), at.to_ctx[3], False)
        self.down = copies.remote(part(final), part(final), at.to_ctx[1], False)

    def each(self, body):
        begin, end = self.range

        def one(index, carry):
            body(pl.ds(pl.multiple_of(begin + index * STEP, LANES), STEP))
            return carry

        lax.fori_loop(0, (end - begin) // STEP, one, 0)

    def gather(self):
        half = self.pair.shape[0] // 2

        @pl.when(self.at.outer)
        def _():
            def add(cols):
                top, low = self.values(cols)
                self.pair[:half, cols] = top.astype(BF16)
                self.pair[half:, cols] = low.astype(BF16)

            self.each(add)
            self.up.start()

    def join(self):
        half = self.pair.shape[0] // 2

        @pl.when(self.at.inner)
        def _():
            self.up.wait_recv()

            def add(cols):
                top, low = self.values(cols)
                self.pair[:half, cols] = (top + self.outer_in[:half, cols].astype(F32)).astype(BF16)
                self.pair[half:, cols] = (low + self.outer_in[half:, cols].astype(F32)).astype(BF16)

            self.each(add)
            self.across.start()

    def share(self):
        @pl.when(self.at.inner)
        def _():
            self.across.wait_recv()

            def add(cols):
                self.final[:, cols] = (
                    self.pair[:, cols].astype(F32) + self.inner_in[:, cols].astype(F32)
                ).astype(BF16)

            self.each(add)
            self.down.start()

    def finish(self):
        @pl.when(self.at.outer)
        def _():
            self.up.wait_send()
            self.down.wait_recv()

        @pl.when(self.at.inner)
        def _():
            self.across.wait_send()
            self.down.wait_send()

    @staticmethod
    def scratch(rows, columns):
        return [pltpu.VMEM((rows, columns), BF16)] * 3


def chunks(tokens, size=256):
    return [slice(start, start + size) for start in range(0, tokens, size)]


def as_f32(ref, index, rows=slice(None)):
    return ref[index, rows].astype(F32)


def take_mixed(got, mixed, at, heads):
    tokens = mixed.shape[0]
    if heads == 4:
        half = tokens // 2
        for tile in range(2):
            cols = slice(tile * LANES, (tile + 1) * LANES)
            one, two = as_f32(got, 2 * tile), as_f32(got, 2 * tile + 1)
            mixed[:half, cols] = lane_pair((one, 0), (two, 0)).astype(BF16)
            mixed[half:, cols] = lane_pair((one, 1), (two, 1)).astype(BF16)
        return
    for tile in range(2):
        cols = slice(tile * LANES, (tile + 1) * LANES)
        mixed[:, cols] = lane_pair(
            (as_f32(got, 2 * tile), 1), (as_f32(got, 2 * tile + 1), 1)
        ).astype(BF16)
    part = at.here // 2
    mixed[:, 2 * LANES :] = lane_pair((as_f32(got, part), 0), (as_f32(got, part + 2), 0)).astype(BF16)


def write_grad_o(grad, out, heads):
    tokens = grad.shape[0]
    half = tokens // 2
    for c in range(4):
        if heads == 4:
            out[c] = lane_pair(
                head_tile(grad, 0, c, slice(0, half)), head_tile(grad, 0, c, slice(half, None))
            ).astype(BF16)
        else:
            out[c] = lane_pair(head_tile(grad, 0, 4 + c // 2), head_tile(grad, 0, c)).astype(BF16)


def send_blocks(copies, at, mine, out):
    done = [copies.local(mine.at[at.here], out.at[at.here])]
    for other in at.ctx[1:]:
        done.append(copies.remote(mine.at[other], out.at[at.here], {CTX: other}))
    return done


MIDDLE_IN, MIDDLE_OUT, MIDDLE_SCRATCH = 7, 5, 17


def middle_kernel(*refs):
    at = partners()
    ins = [refs[:MIDDLE_IN], refs[MIDDLE_IN : 2 * MIDDLE_IN]]
    refs = refs[2 * MIDDLE_IN :]
    outs = [refs[:MIDDLE_OUT], refs[MIDDLE_OUT : 2 * MIDDLE_OUT]]
    refs = refs[2 * MIDDLE_OUT :]
    scratch = [refs[:MIDDLE_SCRATCH], refs[MIDDLE_SCRATCH : 2 * MIDDLE_SCRATCH]]
    arrivals = refs[2 * MIDDLE_SCRATCH : 2 * MIDDLE_SCRATCH + 4]
    copies = Copies(*refs[2 * MIDDLE_SCRATCH + 4 :])
    streams = []
    for in_refs, out_refs, own in zip(ins, outs, scratch):
        s = Bag()
        s.o, s.x, s.dy, s.small, proj_in, up_in, down_in = in_refs
        s.y, s.dmid, s.do_out, s.rest_out, s.sums = out_refs
        (
            s.proj, s.up, s.down, s.rest, s.mixed, s.part, s.part_in, s.mid, s.first, s.first_t, s.dy_t,
            s.act, s.dz, s.grad, s.grad_in, s.do, s.do_mine,
        ) = own
        s.heads = proj_in.shape[1] // HD
        s.proj_done = copies.local(proj_in, s.proj)
        s.rest_done = [copies.local(up_in, s.up), copies.local(down_in, s.down)]
        streams.append(s)
    text, image = streams
    meet([at.to_x, at.to_y] + at.to_ctx[1:] + [at.to_core])

    def project(s):
        take_mixed(s.o, s.mixed, at, s.heads)
        s.proj_done.wait()
        for cols in chunks(s.x.shape[1]):
            s.part[:, cols] = dot(s.mixed[...], s.proj[cols, :], ((1,), (1,)))
        s.part_done = copies.remote(s.part, s.part_in, at.to_core)
        s.sums[...] = jnp.zeros_like(s.sums)
        for rows in chunks(s.dy.shape[0]):
            s.dy_t[:, rows] = jnp.transpose(s.dy[rows, :])

    def second_norm(s):
        s.part_done.wait()
        for rows in chunks(s.x.shape[0]):
            middle = (
                s.x[rows, :].astype(F32) + s.part[rows, :] + s.part_in[rows, :] + s.small[3:4]
            )
            s.mid[rows, :] = middle
            normed, _ = normalise(middle)
            low = (normed * s.small[1:2] + s.small[4:5]).astype(BF16)
            s.first[rows, :] = low
            s.first_t[:, rows] = jnp.transpose(low)

    def feed_forward(s):
        tokens, width = s.x.shape
        hidden, own = s.up.shape[1], s.proj.shape[1]
        for copy in s.rest_done:
            copy.wait()

        def tile(index, carry):
            cols = pl.ds(pl.multiple_of(index * 256, 256), 256)
            up, down = s.up[:, cols], s.down[:, cols]
            per_row = width // 256
            up_cols = pl.ds(pl.multiple_of(own + index * 256, LANES), 256)
            down_cols = pl.ds(pl.multiple_of(own + hidden + index * 256, LANES), 256)
            row = pl.ds(7 + index // per_row, 1)
            place = pl.ds(pl.multiple_of((index % per_row) * 256, 256), 256)
            bias = s.small[row, place]
            total = jnp.zeros((1, 256), F32)
            for rows in chunks(tokens):
                z = dot(s.first[rows, :], up) + bias
                sg = jax.nn.sigmoid(1.702 * z)
                zs = z * sg
                s.act[rows, cols] = zs.astype(BF16)
                grad = dot(s.dy[rows, :], down)
                low = (grad * (sg + 1.702 * zs * (1.0 - sg))).astype(BF16)
                s.dz[rows, cols] = low
                total = total + jnp.sum(low.astype(F32), axis=0, keepdims=True)
            s.sums[row, place] = total
            s.rest[:, up_cols] = dot(s.first_t[...], s.dz[:, cols]).astype(BF16)
            s.rest[:, down_cols] = dot(s.dy_t[...], s.act[:, cols]).astype(BF16)
            return carry

        lax.fori_loop(0, hidden // 256, tile, 0)
        for cols in chunks(width):
            s.grad[0, :, cols] = dot(s.dz[...], s.up[cols, :], ((1,), (1,)))
        s.grad_done = copies.remote(s.grad.at[0], s.grad_in.at[0], at.to_core)
        for cols in chunks(width):
            s.grad[1, :, cols] = dot(s.act[...], s.down[cols, :], ((1,), (1,)))
        s.y_done = copies.remote(s.grad.at[1], s.grad_in.at[1], at.to_core)

    def back(s):
        sums = s.sums
        s.grad_done.wait()
        for rows in chunks(s.x.shape[0]):
            normed, inv = normalise(s.mid[rows, :])
            second = s.grad[0, rows, :] + s.grad_in[0, rows, :]
            scaled = second * s.small[1:2]
            dy = s.dy[rows, :].astype(F32)
            dmid = dy + inv * (
                scaled
                - jnp.mean(scaled, axis=-1, keepdims=True)
                - normed * jnp.mean(scaled * normed, axis=-1, keepdims=True)
            )
            s.dmid[rows, :] = dmid
            sums[1:2] += jnp.sum(second * normed, axis=0, keepdims=True)
            sums[3:4] += jnp.sum(dmid, axis=0, keepdims=True)
            sums[4:5] += jnp.sum(second, axis=0, keepdims=True)
            sums[5:6] += jnp.sum(dy, axis=0, keepdims=True)
            low = dmid.astype(BF16)
            s.first_t[:, rows] = jnp.transpose(low)
            s.do[rows, :] = dot(low, s.proj[...])
        write_grad_o(s.do, s.do_mine, s.heads)
        s.do_done = send_blocks(copies, at, s.do_mine, s.do_out)
        s.rest[:, : s.proj.shape[1]] = dot(s.first_t[...], s.mixed[...]).astype(BF16)

    def output(s):
        s.y_done.wait()
        for rows in chunks(s.x.shape[0]):
            s.y[rows, :] = (
                s.mid[rows, :] + s.grad[1, rows, :] + s.grad_in[1, rows, :] + s.small[5:6]
            ).astype(BF16)

    project(text)
    project(image)
    second_norm(text)
    feed_forward(text)
    second_norm(image)
    back(text)
    plane = PlaneSum(copies, at, text.rest, arrivals)
    feed_forward(image)
    back(image)
    keep = copies.local(image.rest, image.rest_out)
    plane.cross()
    output(text)
    output(image)
    plane.arrived()
    half = plane.half

    def put(cols):
        text.rest_out[:half, cols], text.rest_out[half:, cols] = plane.halves(cols)

    by_columns(plane.columns, put)
    plane.sent()
    keep.wait()
    for s in streams:
        for copy in s.do_done:
            copy.wait()


def middle(streams):
    vmem, hbm = pl.BlockSpec(memory_space=pltpu.VMEM), pl.BlockSpec(memory_space=pl.ANY)
    out_shape, out_specs, scratch = [], [], []
    arrivals = None
    for o, x, dy, small, proj, up, down in streams:
        tokens, width = x.shape
        hidden, own = up.shape[1], proj.shape[1]
        rest = (width, own + 2 * hidden)
        summed = arrivals is None
        if summed:
            arrivals = PlaneSum.arrivals(width // 4, rest[1])
        out_shape += [
            jax.ShapeDtypeStruct((tokens, width), BF16),
            jax.ShapeDtypeStruct((tokens, width), F32),
            jax.ShapeDtypeStruct(o.shape, BF16),
            jax.ShapeDtypeStruct((width // 4, rest[1]), F32)
            if summed
            else jax.ShapeDtypeStruct(rest, BF16),
            jax.ShapeDtypeStruct(small.shape, F32),
        ]
        out_specs += [vmem, vmem, hbm, vmem if summed else hbm, vmem]
        scratch += [
            pltpu.VMEM(proj.shape, BF16),
            pltpu.VMEM(up.shape, BF16),
            pltpu.VMEM(down.shape, BF16),
            pltpu.VMEM(rest, BF16),
            pltpu.VMEM((tokens, own), BF16),
            pltpu.VMEM((tokens, width), F32),
            pltpu.VMEM((tokens, width), F32),
            pltpu.VMEM((tokens, width), F32),
            pltpu.VMEM((tokens, width), BF16),
            pltpu.VMEM((width, tokens), BF16),
            pltpu.VMEM((width, tokens), BF16),
            pltpu.VMEM((tokens, hidden), BF16),
            pltpu.VMEM((tokens, hidden), BF16),
            pltpu.VMEM((2, tokens, width), F32),
            pltpu.VMEM((2, tokens, width), F32),
            pltpu.VMEM((tokens, own), F32),
            pltpu.VMEM(o.shape, BF16),
        ]
    results = pl.pallas_call(
        middle_kernel,
        out_shape=out_shape,
        in_specs=([vmem] * 4 + [hbm] * 3) * 2,
        out_specs=out_specs,
        scratch_shapes=scratch + arrivals + copy_sems(2 * 6 + 6, 2 * 4 + 1),
        compiler_params=pltpu.CompilerParams(
            collective_id=1, has_side_effects=True, vmem_limit_bytes=64 * 1024 * 1000
        ),
        name="middle",
    )(*streams[0], *streams[1])
    return results[:MIDDLE_OUT], results[MIDDLE_OUT:]


def take_dqkv(got, out, at, heads):
    tokens, width = out.shape[0], heads * HD

    def put(which, tile, rows, low, high):
        start = which * width + tile * LANES
        out[rows, start : start + LANES] = lane_pair(low, high).astype(BF16)

    every = slice(None)
    if heads == 4:
        half = tokens // 2
        top, low, keys = slice(0, half), slice(half, tokens), slice(half, half + tokens)
        for tile in range(2):
            one, two = 2 * tile, 2 * tile + 1
            for side, rows in ((0, top), (1, low)):
                put(0, tile, rows, (as_f32(got, one, top), side), (as_f32(got, two, top), side))
            for which in (1, 2):
                side = which - 1
                put(which, tile, every, (as_f32(got, one, keys), side), (as_f32(got, two, keys), side))
        return

    def part(position, index):
        return got[position, index].astype(F32)

    for tile in range(2):
        one, two = 2 * tile, 2 * tile + 1
        put(0, tile, every, (part(one, 0), 0), (part(two, 0), 0))
        put(1, tile, every, (part(one, 1), 0), (part(two, 1), 0))
        put(2, tile, every, (part(one, 1), 1), (part(two, 1), 1))
    put(0, 2, every, (part(at.here_high, 0), 1), (part(at.here_high + 2, 0), 1))
    one, two = part(0, 2) + part(1, 2), part(2, 2) + part(3, 2)
    put(1, 2, every, (one, 1), (two, 1))
    put(2, 2, every, (one, 0), (two, 0))


LAST_IN, LAST_OUT, LAST_SCRATCH = 12, 4, 18


def last_kernel(*refs):
    at = partners()
    ins = [refs[:LAST_IN], refs[LAST_IN : 2 * LAST_IN]]
    refs = refs[2 * LAST_IN :]
    outs = [refs[:LAST_OUT], refs[LAST_OUT : 2 * LAST_OUT]]
    refs = refs[2 * LAST_OUT :]
    count = LAST_SCRATCH + 10
    scratch = [refs[:count], refs[count : 2 * count]]
    refs = refs[2 * count :]
    rest_arrivals, rest_loads = refs[:4], refs[4:7]
    copies = Copies(*refs[7:])
    streams = []
    for in_refs, out_refs, own in zip(ins, outs, scratch):
        s = Bag()
        (
            s.m_in, s.do_in, s.o_in, s.lse, s.seg_row, s.first_in, s.x_in, s.small, s.weight_in, s.dmid_in,
            s.rest, s.sums_in,
        ) = in_refs
        s.grad_rows, s.sums, s.rest_final, s.qkv_final = out_refs
        (
            s.m, s.do, s.o, s.seg_col, s.acc, s.back, s.got, s.dqkv, s.weight, s.first, s.x, s.dmid,
            s.part, s.part_in, s.g_qkv, s.sums_own, s.sums_out, s.sums_got,
        ) = own[:LAST_SCRATCH]
        s.rest_line, s.qkv_line = own[LAST_SCRATCH : LAST_SCRATCH + 3], own[LAST_SCRATCH + 3 : LAST_SCRATCH + 6]
        s.qkv_arrivals = own[LAST_SCRATCH + 6 :]
        s.heads = s.weight.shape[2] // HD
        s.reads = [
            copies.local(src, dst) for src, dst in ((s.m_in, s.m), (s.do_in, s.do), (s.o_in, s.o))
        ]
        streams.append(s)
    text, image = streams
    meet([at.to_x, at.to_y] + at.to_ctx[1:] + [at.to_core])
    plane = PlaneSum(copies, at, image.rest, rest_arrivals, rest_loads)
    text_half = text.rest.shape[0] // 2

    def text_values(cols):
        return text.rest[:text_half, cols], text.rest[text_half:, cols]

    text_line = LineSum(
        copies, at, text_values, text.rest_line, text.rest_final, 0, text.rest.shape[1]
    )
    text_line.gather()
    for s in (image, text):
        document_columns(s.seg_row, s.seg_col)
    for s in streams:
        s.loads = [
            copies.local(src, dst)
            for src, dst in (
                (s.weight_in, s.weight), (s.first_in, s.first), (s.x_in, s.x), (s.dmid_in, s.dmid),
            )
        ]
    image.acc[...] = jnp.zeros_like(image.acc)
    image.back[...] = jnp.zeros_like(image.back)
    for s in (image, text):
        for copy in s.reads:
            copy.wait()

    def image_tasks(begin, end):
        s = image
        unattend_image(at, s.m, s.do, s.o, s.lse, s.seg_col, s.seg_row, s.acc, s.back, begin, end)

    image_tasks(0, 6)
    text_line.join()
    image_tasks(6, 12)
    for source in range(4):
        image.back[source, 1] = image.acc[0, key_range(source)].astype(BF16)
        image.back[source, 2] = image.acc[1, key_range(source)].astype(BF16)
    image.sends = send_blocks(copies, at, image.back, image.got)
    text_line.share()
    s = text
    unattend_text(s.m, s.do, s.o, s.lse, s.seg_col, s.seg_row, s.acc.at[0], s.back)
    text.sends = send_blocks(copies, at, text.back, text.got)
    plane.cross()

    def project(s):
        width = s.x.shape[1]
        own = s.heads * HD
        for copy in s.sends:
            copy.wait()
        for copy in s.loads:
            copy.wait()
        take_dqkv(s.got, s.dqkv, at, s.heads)
        for which in range(3):
            cols = slice(which * own, (which + 1) * own)
            s.g_qkv[:, cols] = dot(s.first[...], s.dqkv[:, cols]).astype(BF16)
        s.qkv_plane = PlaneSum(copies, at, s.g_qkv, s.qkv_arrivals)
        for cols in chunks(width):
            total = dot(s.dqkv[:, :own], s.weight[0, cols, :], ((1,), (1,)))
            total = total + dot(s.dqkv[:, own : 2 * own], s.weight[1, cols, :], ((1,), (1,)))
            s.part[:, cols] = total + dot(s.dqkv[:, 2 * own :], s.weight[2, cols, :], ((1,), (1,)))
        s.part_done = copies.remote(s.part, s.part_in, at.to_core)
        s.sums_own[...] = s.sums_in[...]
        s.sums_own[6:7, :own] = jnp.sum(s.dqkv[:, :own].astype(F32), axis=0, keepdims=True)
        s.sums_own[6:7, own:] = jnp.sum(s.dqkv[:, 2 * own :].astype(F32), axis=0, keepdims=True)
        s.qkv_sum = LineSum(
            copies, at, s.qkv_plane.halves, s.qkv_line, s.qkv_final, 0, 3 * own
        )

    def input_grad(s):
        s.part_done.wait()
        for rows in chunks(s.x.shape[0]):
            normed, inv = normalise(s.x[rows, :].astype(F32))
            first = s.part[rows, :] + s.part_in[rows, :]
            scaled = first * s.small[0:1]
            s.grad_rows[rows, :] = s.dmid[rows, :] + inv * (
                scaled
                - jnp.mean(scaled, axis=-1, keepdims=True)
                - normed * jnp.mean(scaled * normed, axis=-1, keepdims=True)
            )
            s.sums_own[0:1] += jnp.sum(first * normed, axis=0, keepdims=True)
            s.sums_own[2:3] += jnp.sum(first, axis=0, keepdims=True)
        s.sums_done = [copies.remote(s.sums_own, s.sums_got.at[0], at.to_x)]

    def add_sums(s, step):
        s.sums_done[-1].wait_recv()
        before = s.sums_own if step == 0 else s.sums_out.at[step - 1]
        after = s.sums if step == 3 else s.sums_out.at[step]
        after[...] = before[...] + s.sums_got[step]
        if step < 3:
            device = (at.to_y, at.to_ctx[1], at.to_ctx[2])[step]
            s.sums_done.append(copies.remote(after, s.sums_got.at[step + 1], device))

    project(image)
    plane.arrived()
    middle_column = plane.columns // (2 * STEP) * STEP
    rest_lines = [
        LineSum(copies, at, plane.halves, image.rest_line, image.rest_final, begin, end)
        for begin, end in ((0, middle_column), (middle_column, plane.columns))
    ]
    rest_lines[0].gather()
    input_grad(image)
    image.qkv_plane.cross()
    rest_lines[1].gather()
    project(text)
    rest_lines[0].join()
    input_grad(text)
    text.qkv_plane.cross()
    image.qkv_plane.arrived()
    image.qkv_sum.gather()
    rest_lines[1].join()
    add_sums(image, 0)
    rest_lines[0].share()
    add_sums(text, 0)
    text.qkv_plane.arrived()
    text.qkv_sum.gather()
    image.qkv_sum.join()
    add_sums(image, 1)
    add_sums(text, 1)
    rest_lines[1].share()
    text.qkv_sum.join()
    add_sums(image, 2)
    add_sums(text, 2)
    image.qkv_sum.share()
    text.qkv_sum.share()
    add_sums(image, 3)
    add_sums(text, 3)
    for line in [text_line] + rest_lines + [image.qkv_sum, text.qkv_sum]:
        line.finish()
    plane.sent()
    for s in streams:
        s.qkv_plane.sent()
        for copy in s.sums_done:
            copy.wait_send()


def last(streams):
    vmem, hbm = pl.BlockSpec(memory_space=pltpu.VMEM), pl.BlockSpec(memory_space=pl.ANY)
    out_shape, scratch = [], []
    for messages, do, o, lse, seg, first, x, small, weight, dmid, rest, sums in streams:
        tokens, width = x.shape
        own = weight.shape[2]
        rest_shape, qkv_shape = (width // 4, rest.shape[1]), (width // 4, 3 * own)
        out_shape += [
            jax.ShapeDtypeStruct((tokens, width), F32),
            jax.ShapeDtypeStruct(small.shape, F32),
            jax.ShapeDtypeStruct(rest_shape, BF16),
            jax.ShapeDtypeStruct(qkv_shape, BF16),
        ]
        scratch += [
            pltpu.VMEM(messages.shape, BF16),
            pltpu.VMEM(do.shape, BF16),
            pltpu.VMEM(do.shape, BF16),
            pltpu.VMEM((4 * tokens, LANES), F32),
            pltpu.VMEM((1 if own == 4 * HD else 2, 4 * tokens, LANES), F32),
            pltpu.VMEM(messages.shape, BF16),
            pltpu.VMEM(messages.shape, BF16),
            pltpu.VMEM((tokens, 3 * own), BF16),
            pltpu.VMEM(weight.shape, BF16),
            pltpu.VMEM(first.shape, BF16),
            pltpu.VMEM((tokens, width), BF16),
            pltpu.VMEM((tokens, width), F32),
            pltpu.VMEM((tokens, width), F32),
            pltpu.VMEM((tokens, width), F32),
            pltpu.VMEM((width, 3 * own), BF16),
            pltpu.VMEM(small.shape, F32),
            pltpu.VMEM((3,) + small.shape, F32),
            pltpu.VMEM((4,) + small.shape, F32),
        ]
        scratch += LineSum.scratch(*rest_shape) + LineSum.scratch(*qkv_shape)
        scratch += PlaneSum.arrivals(*qkv_shape)
    scratch += PlaneSum.arrivals(*rest_shape) + PlaneSum.loads_scratch(*rest_shape)
    specs = [hbm, hbm, hbm, vmem, vmem, hbm, hbm, vmem, hbm, hbm, vmem, vmem]
    specs += specs[:10] + [hbm, vmem]
    results = pl.pallas_call(
        last_kernel,
        out_shape=out_shape,
        in_specs=specs,
        out_specs=[vmem] * 8,
        scratch_shapes=scratch + copy_sems(2 * (3 + 1 + 4 + 6) + 6 + 3 * 5, 2 * (1 + 7) + 3),
        compiler_params=pltpu.CompilerParams(
            collective_id=2, has_side_effects=True, vmem_limit_bytes=64 * 1024 * 1000
        ),
        name="last",
    )(*streams[0], *streams[1])
    return results[:4], results[4:]


def take_own(group, row):
    columns = row.shape[1] // 4
    return pltpu.roll(row, (4 - group) % 4 * columns, 1)[:, :columns]


def finish_kernel(*refs):
    ins = [refs[:3], refs[3:6]]
    outs = [refs[6:13], refs[13:]]
    for (sums, rest, qkv), (gains, shifts, bias, qkv_out, proj, up, down) in zip(ins, outs):
        group = lax.axis_index(FSDP)
        rows = take_own(group, sums[0:8])
        gains[...] = rows[0:2]
        shifts[...] = rows[2:6]
        line = jnp.concatenate([sums[6:7], sums[7:8], sums[8:9]], axis=1)
        bias[...] = take_own(group, jnp.broadcast_to(line, (8, line.shape[1])))[0:1]
        own = qkv.shape[1] // 3
        for which in range(3):
            qkv_out[which] = qkv[:, which * own : (which + 1) * own].astype(F32)
        hidden = up.shape[1]
        up[...] = rest[:, own : own + hidden].astype(F32)
        if down.shape[0] > down.shape[1]:
            proj[...] = jnp.transpose(rest[:, :own].astype(F32))
            down[...] = jnp.transpose(rest[:, own + hidden :].astype(F32))
        else:
            proj[...] = rest[:, :own].astype(F32)
            down[...] = rest[:, own + hidden :].astype(F32)


def finish(streams):
    out_shape = []
    for sums, rest, qkv, flip in streams:
        rows, own = qkv.shape[0], qkv.shape[1] // 3
        hidden = (rest.shape[1] - own) // 2
        shapes = [(2, rows), (4, rows), (1, 3 * rows), (3, rows, own)]
        shapes += [(own, rows), (rows, hidden), (hidden, rows)] if flip else [
            (rows, own), (rows, hidden), (rows, hidden)
        ]
        out_shape += [jax.ShapeDtypeStruct(shape, F32) for shape in shapes]
    results = pl.pallas_call(finish_kernel, out_shape=out_shape, name="finish")(
        *streams[0][:3], *streams[1][:3]
    )
    return results[:7], results[7:]


def on_device(*args):
    streams = []
    for item, causal in ((args[10:], True), (args[:10], False)):
        s = Bag()
        rows, s.seg, cotangent, s.gains, s.shifts, s.head_bias, s.qkv, proj, s.up, down = item
        s.flip, s.x, s.dy = causal, rows[0], cotangent[0]
        s.down, s.proj = (down, proj) if causal else (down.T, proj.T)
        streams.append(s)
    started = front(
        [(s.x, s.seg, s.gains, s.shifts, s.head_bias, s.qkv, s.up, s.down, s.proj) for s in streams]
    )
    for s, (weight, small, first, messages, proj, up, down, o, lse, o_got) in zip(streams, started):
        s.weight, s.small, s.first, s.messages, s.o, s.lse = weight, small, first, messages, o, lse
        s.weights, s.o_got = (proj, up, down), o_got
    done = middle([(s.o_got, s.x, s.dy, s.small, *s.weights) for s in streams])
    ended = last(
        [
            (s.messages, do, s.o, s.lse, s.seg, s.first, s.x, s.small, s.weight, dmid, rest, sums)
            for s, (y, dmid, do, rest, sums) in zip(streams, done)
        ]
    )
    final = finish([(sums, rest, qkv, s.flip) for s, (_, sums, rest, qkv) in zip(streams, ended)])
    outputs = []
    for s, (y, *_), (grad_rows, *_), (gains, shifts, bias, qkv, proj, up, down) in zip(
        streams, done, ended, final
    ):
        if not s.flip:
            proj, down = proj.T, down.T
        outputs.append((y[None], grad_rows[None], gains, shifts, bias, qkv, proj, up, down))
    return outputs[1] + outputs[0]


def layer_stats(rows):
    row_mean = jnp.mean(rows, axis=-1, keepdims=True)
    centred = rows - row_mean
    inv_std = lax.rsqrt(jnp.mean(centred * centred, axis=-1, keepdims=True) + 1e-05)
    return (centred * inv_std, inv_std)


def norm_back(grad_normed_out, normed, inv_std, gain):
    scaled = grad_normed_out * gain
    return inv_std * (
        scaled
        - jnp.mean(scaled, axis=-1, keepdims=True)
        - normed * jnp.mean(scaled * normed, axis=-1, keepdims=True)
    )


def tensor_psum(partial_rows):
    return lax.psum(partial_rows, TP)


def any_mesh_block(
    rows_in,
    seg_row,
    cotangent,
    gains,
    shifts,
    head_bias,
    qkv_weight,
    proj_weight,
    up_weight,
    down_weight,
    causal,
):
    gain_full, shift_full, bias_full, qkv_full, proj_full, up_full, down_full = (
        lax.all_gather(gains, FSDP, axis=1, tiled=True),
        lax.all_gather(shifts, FSDP, axis=1, tiled=True),
        lax.all_gather(head_bias, FSDP, axis=1, tiled=True),
        lax.all_gather(qkv_weight, FSDP, axis=1, tiled=True),
        lax.all_gather(proj_weight, FSDP, axis=1, tiled=True),
        lax.all_gather(up_weight, FSDP, axis=0, tiled=True),
        lax.all_gather(down_weight, FSDP, axis=1, tiled=True),
    )
    gain_vals = gain_full.astype(jnp.float32)
    shift_vals = shift_full.astype(jnp.float32)
    bias_vals = bias_full[0].astype(jnp.float32)
    tp_width = qkv_full.shape[2]
    local_rows = rows_in.shape[1]
    seq_length = seg_row.shape[1]
    head_local = tp_width // HD
    rows = rows_in[0].astype(jnp.float32)
    row_start = lax.axis_index(CTX) * local_rows
    seg_all = seg_row[0]
    seg_query = lax.dynamic_slice_in_dim(seg_all, row_start, local_rows)
    query_pos = row_start + jnp.arange(local_rows, dtype=jnp.int32)
    key_pos = jnp.arange(seq_length, dtype=jnp.int32)
    allowed = seg_query[:, None] == seg_all[None, :]
    if causal:
        allowed = jnp.logical_and(allowed, key_pos[None, :] <= query_pos[:, None])

    def to_heads(matrix):
        return matrix.reshape(matrix.shape[0], head_local, HD).transpose(1, 0, 2)

    def from_heads(stacked):
        return stacked.transpose(1, 0, 2).reshape(stacked.shape[1], head_local * HD)

    normed_one, inv_one = layer_stats(rows)
    first_in = (normed_one * gain_vals[0] + shift_vals[0]).astype(jnp.bfloat16)
    queries = (
        jnp.dot(first_in, qkv_full[0], preferred_element_type=jnp.float32) + bias_vals[:tp_width]
    ).astype(jnp.bfloat16)
    key_rows = jnp.dot(first_in, qkv_full[1], preferred_element_type=jnp.float32).astype(
        jnp.bfloat16
    )
    values = (
        jnp.dot(first_in, qkv_full[2], preferred_element_type=jnp.float32)
        + bias_vals[tp_width : 2 * tp_width]
    ).astype(jnp.bfloat16)
    key_all, value_all = (
        lax.all_gather(key_rows, CTX, axis=0, tiled=True),
        lax.all_gather(values, CTX, axis=0, tiled=True),
    )
    query_heads = to_heads(queries)
    key_heads = to_heads(key_all)
    value_heads = to_heads(value_all)

    def attend(head_items):
        query_h, key_h, value_h = head_items
        scores = dot(query_h, key_h, ((1,), (1,))) * 0.125
        scores = jnp.where(allowed, scores, -1e30)
        row_top = jnp.max(scores, axis=-1, keepdims=True)
        weights = jnp.exp(scores - row_top)
        row_total = jnp.sum(weights, axis=-1, keepdims=True)
        weights_low = (weights / row_total).astype(jnp.bfloat16)
        mixed_h = dot(weights_low, value_h, ((1,), (0,)))
        return (mixed_h.astype(jnp.bfloat16), row_top[:, 0] + jnp.log(row_total[:, 0]))

    mixed_heads, log_totals = lax.map(attend, (query_heads, key_heads, value_heads))
    mixed = from_heads(mixed_heads)
    middle = (
        rows
        + tensor_psum(jnp.dot(mixed, proj_full, preferred_element_type=jnp.float32))
        + shift_vals[1]
    )
    normed_two, inv_two = layer_stats(middle)
    second_in = (normed_two * gain_vals[1] + shift_vals[2]).astype(jnp.bfloat16)
    hidden = (
        jnp.dot(second_in, up_full, preferred_element_type=jnp.float32) + bias_vals[2 * tp_width :]
    )
    sigma = jax.nn.sigmoid(1.702 * hidden)
    activated = (hidden * sigma).astype(jnp.bfloat16)
    output = (
        middle
        + tensor_psum(jnp.dot(activated, down_full, preferred_element_type=jnp.float32))
        + shift_vals[3]
    )
    grad_out = cotangent[0].astype(jnp.float32)
    grad_down_bias = jnp.sum(grad_out, axis=0)
    grad_branch = grad_out.astype(jnp.bfloat16)
    grad_down = dot(activated, grad_branch, ((0,), (0,)))
    grad_act = dot(grad_branch, down_full, ((1,), (1,)))
    grad_hidden = (grad_act * (sigma + 1.702 * hidden * sigma * (1.0 - sigma))).astype(jnp.bfloat16)
    grad_up_bias = jnp.sum(grad_hidden.astype(jnp.float32), axis=0)
    grad_up = dot(second_in, grad_hidden, ((0,), (0,)))
    grad_second = tensor_psum(
        dot(grad_hidden, up_full, ((1,), (1,)))
    )
    grad_gain_two = jnp.sum(grad_second * normed_two, axis=0)
    grad_shift_two = jnp.sum(grad_second, axis=0)
    grad_middle = grad_out + norm_back(grad_second, normed_two, inv_two, gain_vals[1])
    grad_proj_bias = jnp.sum(grad_middle, axis=0)
    grad_attn = grad_middle.astype(jnp.bfloat16)
    grad_proj = dot(mixed, grad_attn, ((0,), (0,)))
    grad_mixed = dot(grad_attn, proj_full, ((1,), (1,))).astype(jnp.bfloat16)

    def attend_back(head_items):
        query_h, key_h, value_h, grad_h, log_total = head_items
        scores = dot(query_h, key_h, ((1,), (1,))) * 0.125
        weights = jnp.where(allowed, jnp.exp(scores - log_total[:, None]), 0.0)
        grad_weights = dot(grad_h, value_h, ((1,), (1,)))
        row_delta = jnp.sum(weights * grad_weights, axis=-1, keepdims=True)
        grad_scores = (weights * (grad_weights - row_delta)).astype(jnp.bfloat16)
        grad_query_h = (
            dot(grad_scores, key_h, ((1,), (0,))) * 0.125
        )
        grad_key_h = (
            dot(grad_scores, query_h, ((0,), (0,)))
            * 0.125
        )
        grad_value_h = dot(weights.astype(jnp.bfloat16), grad_h, ((0,), (0,)))
        return (grad_query_h, grad_key_h, grad_value_h)

    query_parts, key_parts, value_parts = lax.map(
        attend_back, (query_heads, key_heads, value_heads, to_heads(grad_mixed), log_totals)
    )
    key_sum, value_sum = (
        lax.psum_scatter(from_heads(key_parts), CTX, scatter_dimension=0, tiled=True),
        lax.psum_scatter(from_heads(value_parts), CTX, scatter_dimension=0, tiled=True),
    )
    grad_query = from_heads(query_parts).astype(jnp.bfloat16)
    grad_key = key_sum.astype(jnp.bfloat16)
    grad_value = value_sum.astype(jnp.bfloat16)
    grad_qkv = jnp.stack(
        [
            dot(first_in, grad_query, ((0,), (0,))),
            dot(first_in, grad_key, ((0,), (0,))),
            dot(first_in, grad_value, ((0,), (0,))),
        ]
    )
    grad_head = jnp.concatenate(
        [
            jnp.sum(grad_query.astype(jnp.float32), axis=0),
            jnp.sum(grad_value.astype(jnp.float32), axis=0),
            grad_up_bias,
        ]
    )[None, :]
    grad_first_part = dot(grad_query, qkv_full[0], ((1,), (1,)))
    grad_first_part = grad_first_part + dot(grad_key, qkv_full[1], ((1,), (1,)))
    grad_first_part = grad_first_part + dot(grad_value, qkv_full[2], ((1,), (1,)))
    grad_first = tensor_psum(grad_first_part)
    grad_gain_one = jnp.sum(grad_first * normed_one, axis=0)
    grad_shift_one = jnp.sum(grad_first, axis=0)
    grad_rows = grad_middle + norm_back(grad_first, normed_one, inv_one, gain_vals[0])
    grad_gains = jnp.stack([grad_gain_one, grad_gain_two])
    grad_shifts = jnp.stack([grad_shift_one, grad_proj_bias, grad_shift_two, grad_down_bias])
    share_gains, share_shifts, share_head, share_qkv, share_proj, share_up, share_down = (
        lax.psum_scatter(grad_gains, FSDP, scatter_dimension=1, tiled=True),
        lax.psum_scatter(grad_shifts, FSDP, scatter_dimension=1, tiled=True),
        lax.psum_scatter(grad_head, FSDP, scatter_dimension=1, tiled=True),
        lax.psum_scatter(grad_qkv, FSDP, scatter_dimension=1, tiled=True),
        lax.psum_scatter(grad_proj, FSDP, scatter_dimension=1, tiled=True),
        lax.psum_scatter(grad_up, FSDP, scatter_dimension=0, tiled=True),
        lax.psum_scatter(grad_down, FSDP, scatter_dimension=1, tiled=True),
    )
    owned = lax.psum(
        (share_gains, share_shifts, share_head, share_qkv, share_proj, share_up, share_down), CTX
    )
    return (output.astype(jnp.bfloat16)[None], grad_rows[None]) + tuple(owned)


def on_any_mesh(
    image_input,
    image_segments,
    image_cotangent,
    image_gains,
    image_shifts,
    image_head_bias,
    image_qkv_weight,
    image_proj_weight,
    image_up_weight,
    image_down_weight,
    text_input,
    text_segments,
    text_cotangent,
    text_gains,
    text_shifts,
    text_head_bias,
    text_qkv_weight,
    text_proj_weight,
    text_up_weight,
    text_down_weight,
):
    image_results = any_mesh_block(
        image_input,
        image_segments,
        image_cotangent,
        image_gains,
        image_shifts,
        image_head_bias,
        image_qkv_weight,
        image_proj_weight,
        image_up_weight,
        image_down_weight,
        False,
    )
    text_results = any_mesh_block(
        text_input,
        text_segments,
        text_cotangent,
        text_gains,
        text_shifts,
        text_head_bias,
        text_qkv_weight,
        text_proj_weight,
        text_up_weight,
        text_down_weight,
        True,
    )
    return image_results + text_results


def stream_specs():
    return (
        P(FSDP, CTX, None),
        P(FSDP, None),
        P(FSDP, CTX, None),
        P(None, FSDP),
        P(None, FSDP),
        P(TP, FSDP),
        P(None, FSDP, TP),
        P(TP, FSDP),
        P(FSDP, TP),
        P(TP, FSDP),
    )


def solution(mesh):
    one = stream_specs()
    grads = (one[0], one[0]) + one[3:]
    body = on_device
    if (mesh.shape[FSDP], mesh.shape[CTX], mesh.shape[TP]) != (4, 4, 2):
        body = on_any_mesh
    return jax.shard_map(
        body, mesh=mesh, in_specs=one + one, out_specs=grads + grads, check_vma=False
    )
```

profile of v0, /device:TPU:0, one launch (start us, length us, event | category | flops | bytes accessed | tf_op | source)
XLA Modules:
  0.0 318.0 jit_solution(16550085505733246982)
XLA Ops:
  0.7 104.8 %front.1 = (bf16[3,512,256]{2,1,0:T(8,128)(2,1)}, f32[16,512]{1,0:T(8,128)}, bf16[512,512]{1,0:T(8,128)(2,1)}, bf16[4,768,128]{2,1,0:T(8,128)(2,1)}, bf16[512,25...) custom-call(bf16[512,512]{1,0:T(8,128)(2,1)} %bitcast.15, ...), custom_call_target="tpu_custom_call" | custom-call | tf_op jit(solution)/shard_map/front/pallas_call | solution.py:506
  105.4 43.1 %middle.1 = (bf16[512,512]{1,0:T(8,128)(2,1)}, f32[512,512]{1,0:T(8,128)}, bf16[4,256,128]{2,1,0:T(8,128)(2,1)}, f32[128,2304]{1,0:T(8,128)}, f32[16,512]{1,0:T(...) custom-call(bf16[4,256,128]{2,1,0:T(8,128)(2,1)} %get-tuple-element., ...), custom_call_target="tpu_custom_call" | custom-call | tf_op jit(solution)/shard_map/middle/pallas_call | solution.py:920
  148.5 160.9 %last.1 = (f32[512,512]{1,0:T(8,128)}, f32[16,512]{1,0:T(8,128)}, bf16[128,2304]{1,0:T(8,128)(2,1)}, bf16[128,768]{1,0:T(8,128)(2,1)}, f32[512,768]{1,0:T(8,128)...) custom-call(bf16[4,768,128]{2,1,0:T(8,128)(2,1)} %get-tuple-element.81.refs_0_, ...), custom_call_target="tpu_custom_call" | custom-call | tf_op jit(solution)/shard_map/last/pallas_call | solution.py:1174
  309.5 0.0 copy-start.2
  309.5 0.0 copy-start
  309.5 4.4 %finish.1 = (f32[2,128]{1,0:T(2,128)}, f32[4,128]{1,0:T(4,128)}, f32[1,384]{1,0:T(1,128)}, f32[3,128,256]{2,1,0:T(8,128)}, f32[256,128]{1,0:T(8,128)}, /*index=5...) custom-call(f32[16,512]{1,0:T(8,128)} %get-tuple-element.100.refs_0_, ...), custom_call_target="tpu_custom_call" | custom-call | tf_op jit(solution)/shard_map/finish/pallas_call | solution.py:1226
  313.8 0.0 copy-done.2
  313.8 0.9 copy.42
  314.7 0.0 copy-done
  314.7 0.0 copy-start.3
  314.7 0.0 copy-start.1
  314.7 1.1 copy.43
  315.9 0.2 copy-done.3
  316.1 0.8 copy.44
  316.9 0.0 copy-done.1
  316.9 1.0 copy.45
Async XLA Ops:
  309.5 4.4 %copy-start.2 = (bf16[512,768]{1,0:T(8,128)(2,1)S(1)}, bf16[512,768]{1,0:T(8,128)(2,1)}, u32[]{:S(2)}) copy-start(bf16[512,768]{1,0:T(8,128)(2,1)} %get-tuple-element.80) | copy-start | bytes 2359300
  309.5 5.3 %copy-start = (f32[512,768]{1,0:T(8,128)S(1)}, f32[512,768]{1,0:T(8,128)}, u32[]{:S(2)}) copy-start(f32[512,768]{1,0:T(8,128)} %get-tuple-element.99) | copy-start | bytes 4718596
  314.7 1.4 copy-start.3
  314.7 2.2 copy-start.1
where the time goes:
time: 322 us; the launch traced here: 318 us
  Pallas kernels  313 us (97%)
  local copies, waits for them, and re-layouts  4.03 us (1%)
    pallas_call x1, Pallas kernels, last(): pl.pallas_call(last_kernel, out_shape=out_shape, in_specs=specs, out_spec...  161 us
    pallas_call x1, Pallas kernels, front(): pl.pallas_call(front_kernel, out_shape=out_shape, in_specs=[vmem] * (2 *...  105 us
    pallas_call x1, Pallas kernels, middle(): pl.pallas_call(middle_kernel, out_shape=out_shape, in_specs=([vmem] * 4 +...  43.1 us

commit v1 on v0

--- a/solution.py
+++ b/solution.py
@@ -29,10 +29,13 @@
     return first, second
 
 
-def document_columns(row_ref, out_ref):
-    for start in range(0, out_ref.shape[0], LANES):
+def document_features(row_ref, query_out, key_out):
+    lane = lax.broadcasted_iota(jnp.int32, (LANES, LANES), 1) % HD
+    for start in range(0, query_out.shape[0], LANES):
         row = row_ref[:, start : start + LANES].astype(F32)
-        out_ref[start : start + LANES, :] = jnp.transpose(jnp.broadcast_to(row, (LANES, LANES)))
+        same = jnp.transpose(jnp.broadcast_to(row, (LANES, LANES))) == lane.astype(F32)
+        query_out[start : start + LANES, :] = jnp.where(same, 1.0, 0.0).astype(BF16)
+        key_out[start : start + LANES, :] = jnp.where(same, 0.0, NEG).astype(BF16)
 
 
 def swap_halves(value):
@@ -43,172 +46,119 @@
     return slice(index * KB, (index + 1) * KB)
 
 
-def mix_rows(query, seg_query, keys, seg_keys, own, other, diagonal=None):
-    query = query * own
+def pick(flag, one, zero):
+    return jnp.where(flag == 1, one, zero)
+
+
+def query_rows(head):
+    return pl.ds(pl.multiple_of(head * (QB + 2 * KB), QB), QB)
+
+
+def key_rows(head):
+    return pl.ds(pl.multiple_of(QB + head * KB, QB), KB)
+
+
+def mark_keys(m, features, heads, score_keys, value_keys):
+    first, second = lane_marks()
+    for head in range(heads):
+        for index in range(4):
+            block = m[index, key_rows(head)]
+            score_keys[head, key_range(index)] = block * first + features[key_range(index), :] * second
+            if value_keys is not None:
+                value_keys[head, key_range(index)] = block * second + first
+
+
+def later(index, shape, axis, query_start):
+    key_pos = index * KB + lax.broadcasted_iota(jnp.int32, shape, axis)
+    query_pos = query_start + lax.broadcasted_iota(jnp.int32, shape, 1 - axis)
+    return key_pos > query_pos
+
+
+def mix_rows(query, score_keys, value_keys, head, blocks, query_start=None):
     scores = []
-    for block, seg in zip(keys, seg_keys):
-        score = dot(query, block, ((1,), (1,)))
-        ok = seg_query == seg.astype(F32)
-        if diagonal is not None and len(scores) == len(keys) - 1:
-            key_pos = lax.broadcasted_iota(jnp.int32, score.shape, 1)
-            query_pos = diagonal + lax.broadcasted_iota(jnp.int32, score.shape, 0)
-            ok = jnp.logical_and(ok, key_pos <= query_pos)
-        scores.append(jnp.where(ok, score, NEG))
+    for index in range(blocks):
+        score = dot(query, score_keys[head, key_range(index)], ((1,), (1,)))
+        if query_start is not None:
+            score = jnp.where(later(index, score.shape, 1, query_start), NEG, score)
+        scores.append(score)
     top = jnp.max(functools.reduce(jnp.maximum, scores), axis=1, keepdims=True)
     acc = jnp.zeros((query.shape[0], LANES), F32)
-    for score, block in zip(scores, keys):
-        acc = acc + dot(jnp.exp(score - top).astype(BF16), block * other + own)
+    for index, score in enumerate(scores):
+        acc = acc + dot(jnp.exp(score - top).astype(BF16), value_keys[head, key_range(index)])
     return acc / swap_halves(acc), top + jnp.log(acc)
 
 
-def pick(flag, one, zero):
-    return jnp.where(flag == 1, one, zero)
-
-
-def attend_text(m, seg_col, seg_row, o, lse):
+def text_task(at, task):
+    return 0, task // 2, task % 2
+
+
+def image_task(at, task):
+    shared = 1 - (task + 8) // 12
+    return shared, pick(shared, at.here_high * 2 + task // 2, task // 2 - 2), task % 2
+
+
+def attend(at, m, features, score_keys, value_keys, o, lse, task_of, begin, end, blocks, causal):
     first, second = lane_marks()
     lane = lax.broadcasted_iota(jnp.int32, (QB, LANES), 1)
-    o[...] = jnp.zeros_like(o)
-    for source in range(4):
-        keys = [m[i, QB:] for i in range(source + 1)]
-        segs = [seg_row[:, key_range(i)] for i in range(source + 1)]
-
-        def one(half, carry, source=source, keys=keys, segs=segs):
-            query = m[source, :QB].astype(F32)
-            query = pick(half, swap_halves(query), query).astype(BF16)
-            tokens = pl.ds(pl.multiple_of(source * KB + half * QB, QB), QB)
-            mixed, log_total = mix_rows(
-                query, seg_col[tokens, :1], keys, segs, first, second, half * QB
-            )
-            lse[2 * source + half, :8] = jnp.transpose(log_total)[:8]
-            mixed = pick(half, mixed, swap_halves(mixed))
-            o[source] = jnp.where(lane // HD == half, mixed.astype(BF16), o[source])
-            return carry
-
-        lax.fori_loop(0, 2, one, 0)
-
-
-def image_task(at, task):
-    extra = 1 - (task + 8) // 12
-    block = pick(extra, at.here_low * 4 + task, task - 4)
-    source, half = block // 2, block % 2
-    rows = pl.ds(pl.multiple_of(half * QB, QB), QB)
-    tokens = pl.ds(pl.multiple_of(block * QB, QB), QB)
-    return extra, block, source, rows, tokens
-
-
-def task_marks(extra):
-    first, second = lane_marks()
-    return pick(extra, second, first), pick(extra, first, second)
-
-
-def attend_image(at, m, seg_col, seg_row, o, lse):
-    lane = lax.broadcasted_iota(jnp.int32, (QB, LANES), 1)
-    segs = [seg_row[:, key_range(i)] for i in range(4)]
-    o[...] = jnp.zeros_like(o)
 
     def one(task, carry):
-        extra, block, source, rows, tokens = image_task(at, task)
-        own, other = task_marks(extra)
+        head, source, half = task_of(at, task)
+        start = (source * 2 + half) * QB
+        query = m[source, query_rows(head)].astype(F32)
+        query = pick(half, swap_halves(query), query).astype(BF16)
+        query = query * first + features[pl.ds(pl.multiple_of(start, QB), QB), :] * second
         mixed, log_total = mix_rows(
-            m[source, 0, rows],
-            seg_col[tokens, :1],
-            [m[i, 1 + extra] for i in range(4)],
-            segs,
-            own,
-            other,
+            query, score_keys, value_keys, head, blocks, start if causal else None
         )
-        log_total = jnp.transpose(log_total)
-        lse[block, pl.ds(pl.multiple_of(8 * extra, 8), 8)] = pick(
-            extra, log_total[HD : HD + 8], log_total[:8]
-        )
-        o[source, rows] = jnp.where(lane // HD == 1 - extra, mixed.astype(BF16), o[source, rows])
+        lse[task] = jnp.transpose(log_total)[:8]
+        mixed = pick(half, mixed, swap_halves(mixed)).astype(BF16)
+        rows = pl.ds(pl.multiple_of(head * QB, QB), QB)
+        o[source, rows] = jnp.where(lane // HD == half, mixed, o[source, rows])
         return carry
 
-    lax.fori_loop(0, 12, one, 0)
-
-
-def unmix_rows(query, grad_o, seg_query, keys, seg_keys, totals, lse, delta, own, other, diagonal=None):
-    query, grad_o = query * own, grad_o * other
-    grad_query = jnp.zeros((query.shape[0], LANES), F32)
-    for index, (block, seg, (total, rows)) in enumerate(zip(keys, seg_keys, totals)):
-        score = dot(block, query, ((1,), (1,)))
-        ok = seg == seg_query
-        if diagonal is not None and index == len(keys) - 1:
-            key_pos = lax.broadcasted_iota(jnp.int32, score.shape, 0)
-            query_pos = diagonal + lax.broadcasted_iota(jnp.int32, score.shape, 1)
-            ok = jnp.logical_and(ok, key_pos <= query_pos)
-        weights = jnp.where(ok, jnp.exp(score - lse), 0.0)
-        grad_weights = dot(block, grad_o, ((1,), (1,)))
-        grad_scores = (weights * (grad_weights - delta)).astype(BF16)
-        total[rows, :] += dot(grad_scores, query) + dot(weights.astype(BF16), grad_o)
-        grad_query = grad_query + dot(grad_scores, block, ((0,), (0,)))
-    return grad_query * 0.125
-
-
-def unattend_text(m, do, o, lse, seg_col, seg_row, acc, out):
+    lax.fori_loop(begin, end, one, 0)
+
+
+def unattend(at, m, do, o, lse, features, score_keys, acc, out, task_of, begin, end, blocks, causal):
     first, second = lane_marks()
     lane = lax.broadcasted_iota(jnp.int32, (QB, LANES), 1)
-    acc[...] = jnp.zeros_like(acc)
-    out[:, :QB] = jnp.zeros((4, QB, LANES), BF16)
-    for source in range(4):
-        keys = [m[i, QB:] for i in range(source + 1)]
-        segs = [seg_col[key_range(i), :1] for i in range(source + 1)]
-        totals = [(acc, key_range(i)) for i in range(source + 1)]
-
-        def one(half, carry, source=source, keys=keys, segs=segs, totals=totals):
-            query, grad_o = m[source, :QB].astype(F32), do[source].astype(F32)
-            product = jnp.transpose(grad_o * o[source].astype(F32))
-            query = pick(half, swap_halves(query), query).astype(BF16)
-            grad_o = pick(half, grad_o, swap_halves(grad_o)).astype(BF16)
-            tokens = pl.ds(pl.multiple_of(source * KB + half * QB, QB), QB)
-            grad_query = unmix_rows(
-                query,
-                grad_o,
-                seg_row[:, tokens].astype(F32),
-                keys,
-                segs,
-                totals,
-                lse[2 * source + half, :1],
-                jnp.sum(pick(half, product[HD:], product[:HD]), axis=0, keepdims=True),
-                first,
-                second,
-                half * QB,
-            )
-            grad_query = pick(half, swap_halves(grad_query), grad_query).astype(BF16)
-            out[source, :QB] = jnp.where(lane // HD == half, grad_query, out[source, :QB])
-            return carry
-
-        lax.fori_loop(0, 2, one, 0)
-    for source in range(4):
-        out[source, QB:] = acc[key_range(source)].astype(BF16)
-
-
-def unattend_image(at, m, do, o, lse, seg_col, seg_row, acc, out, begin, end):
-    lane = lax.broadcasted_iota(jnp.int32, (QB, LANES), 1)
-    segs = [seg_col[key_range(i), :1] for i in range(4)]
 
     def one(task, carry):
-        extra, block, source, rows, tokens = image_task(at, task)
-        own, other = task_marks(extra)
-        grad_o = do[source, rows]
-        product = jnp.transpose(grad_o.astype(F32) * o[source, rows].astype(F32))
-        grad_query = unmix_rows(
-            m[source, 0, rows],
-            grad_o,
-            seg_row[:, tokens].astype(F32),
-            [m[i, 1 + extra] for i in range(4)],
-            segs,
-            [(acc.at[extra], key_range(i)) for i in range(4)],
-            lse[block, pl.ds(pl.multiple_of(8 * extra, 8), 8)][:1],
-            jnp.sum(pick(extra, product[:HD], product[HD:]), axis=0, keepdims=True),
-            own,
-            other,
-        ).astype(BF16)
-        out[source, 0, rows] = jnp.where(lane // HD == extra, grad_query, out[source, 0, rows])
+        head, source, half = task_of(at, task)
+        start = (source * 2 + half) * QB
+        rows = pl.ds(pl.multiple_of(head * QB, QB), QB)
+        query, grad_o = m[source, query_rows(head)].astype(F32), do[source, rows].astype(F32)
+        product = jnp.transpose(grad_o * o[source, rows].astype(F32))
+        delta = jnp.sum(pick(half, product[HD:], product[:HD]), axis=0, keepdims=True)
+        query = pick(half, swap_halves(query), query).astype(BF16) * first
+        grad_o = pick(half, grad_o, swap_halves(grad_o)).astype(BF16) * second
+        marked = query + features[pl.ds(pl.multiple_of(start, QB), QB), :] * second
+        row_lse = lse[task, :1]
+        grad_query = jnp.zeros((QB, LANES), F32)
+        for index in range(blocks):
+            keys = m[index, key_rows(head)]
+            score = dot(score_keys[head, key_range(index)], marked, ((1,), (1,)))
+            if causal:
+                score = jnp.where(later(index, score.shape, 0, start), NEG, score)
+            weights = jnp.exp(score - row_lse)
+            grad_weights = dot(keys, grad_o, ((1,), (1,)))
+            grad_scores = (weights * (grad_weights - delta)).astype(BF16)
+            acc[head, key_range(index)] += dot(grad_scores, query) + dot(weights.astype(BF16), grad_o)
+            grad_query = grad_query + dot(grad_scores, keys, ((0,), (0,)))
+        grad_query = grad_query * 0.125
+        grad_query = pick(half, swap_halves(grad_query), grad_query).astype(BF16)
+        out[source, query_rows(head)] = jnp.where(
+            lane // HD == half, grad_query, out[source, query_rows(head)]
+        )
         return carry
 
     lax.fori_loop(begin, end, one, 0)
+
+
+def key_gradients(acc, out):
+    for head in range(acc.shape[0]):
+        for index in range(4):
+            out[index, key_rows(head)] = acc[head, key_range(index)].astype(BF16)
 
 
 class Bag:
@@ -287,6 +237,11 @@
         rows = pl.ds(pl.multiple_of(owner * self.rows + offset, 8), size)
         return self.dst.at[:, rows, :] if len(self.dst.shape) == 3 else self.dst.at[rows, :]
 
+    def near(self):
+        self.own.wait()
+        self.to_x.wait()
+        self.to_y.wait()
+
     def forward(self):
         half = self.rows // 2
         self.to_x.wait_recv()
@@ -325,32 +280,33 @@
     return ref[rows, first : first + LANES], index % 2
 
 
+def halves_pair(ref, start, index):
+    half = ref.shape[0] // 2
+    return lane_pair(
+        head_tile(ref, start, index, slice(0, half)), head_tile(ref, start, index, slice(half, None))
+    ).astype(BF16)
+
+
 def write_messages(qkv, out, heads):
     width = heads * HD
-    tokens = qkv.shape[0]
+
+    def keys_values(index):
+        return lane_pair(head_tile(qkv, width, index), head_tile(qkv, 2 * width, index)).astype(BF16)
+
     for c in range(4):
-        if heads == 4:
-            half = tokens // 2
-            out[c, :half] = lane_pair(
-                head_tile(qkv, 0, c, slice(0, half)), head_tile(qkv, 0, c, slice(half, None))
-            ).astype(BF16)
-            out[c, half:] = lane_pair(
-                head_tile(qkv, width, c), head_tile(qkv, 2 * width, c)
-            ).astype(BF16)
-        else:
-            e = 4 + c // 2
-            out[c, 0] = lane_pair(head_tile(qkv, 0, c), head_tile(qkv, 0, e)).astype(BF16)
-            out[c, 1] = lane_pair(
-                head_tile(qkv, width, c), head_tile(qkv, 2 * width, c)
-            ).astype(BF16)
-            out[c, 2] = lane_pair(
-                head_tile(qkv, 2 * width, e), head_tile(qkv, width, e)
-            ).astype(BF16)
+        out[c, query_rows(0)] = halves_pair(qkv, 0, c)
+        out[c, key_rows(0)] = keys_values(c)
+        if heads == 6:
+            out[c, key_rows(1)] = keys_values(4 + c % 2)
+            out[c, query_rows(1)] = halves_pair(qkv, 0, 4 + c % 2)
 
 
 def message_shape(heads, tokens):
-    part = (tokens // 2 + tokens, LANES) if heads == 4 else (3, tokens, LANES)
-    return (4,) + part
+    return (4, (heads // 2 - 1) * (QB + tokens), LANES)
+
+
+def mixed_shape(heads):
+    return (4, (heads // 2 - 1) * QB, LANES)
 
 
 def first_rows(x_ref, small_ref, weight_ref, first_ref, qkv_ref, step):
@@ -380,7 +336,7 @@
         out[6 + row : 7 + row] = line[0:1, row * width : (row + 1) * width]
 
 
-FRONT_IN, FRONT_OUT, FRONT_SCRATCH = 9, 10, 10
+FRONT_IN, FRONT_OUT, FRONT_SCRATCH = 9, 10, 20
 
 
 def front_kernel(*refs):
@@ -394,15 +350,24 @@
     streams = []
     for in_refs, out_refs, own in zip(ins, outs, scratch):
         s = Bag()
-        s.x, s.seg_row, s.gains, s.shifts, s.bias, s.qkv, s.up, s.down, s.proj = in_refs
+        s.x_in, s.seg_row, s.gains, s.shifts, s.bias, s.qkv, s.up_in, s.down_in, s.proj_in = in_refs
         (
-            s.weight, s.small, s.first, s.messages, s.proj_full, s.up_full, s.down_full, s.o, s.lse,
-            s.o_got,
+            s.weight_out, s.small, s.first_out, s.messages, s.proj_full, s.up_full, s.down_full,
+            s.o_out, s.lse, s.o_got,
         ) = out_refs
         (
-            s.small_in, s.small_own, s.wide, s.flat, s.rows, s.mine, s.got, s.down_t, s.proj_t, s.seg_col,
-        ) = own
+            s.small_in, s.small_own, s.wide, s.flat, s.rows, s.mine, s.got, s.down_t, s.proj_t,
+            s.query_doc, s.key_doc, s.score_keys, s.value_keys, s.x, s.up, s.down, s.proj, s.weight, s.first,
+        ) = own[:19]
+        s.o = own[19]
         s.heads = s.weight.shape[2] // HD
+        s.features = (s.query_doc, s.key_doc)
+        s.reads = [
+            copies.local(src, dst)
+            for src, dst in (
+                (s.x_in, s.x), (s.proj_in, s.proj), (s.up_in, s.up), (s.down_in, s.down),
+            )
+        ]
         streams.append(s)
     meet([at.to_x, at.to_y, at.to_far] + at.to_ctx[1:])
     text, image = streams
@@ -416,10 +381,13 @@
         ]
     image.gather.forward()
     text.gather = Gather(copies, at, text.qkv, text.weight)
+    for s in (image, text):
+        for copy in s.reads:
+            copy.wait()
     text.down_t[...] = jnp.transpose(text.down[...])
     text.proj_t[...] = jnp.transpose(text.proj[...])
     for s in (image, text):
-        document_columns(s.seg_row, s.seg_col)
+        document_features(s.seg_row, *s.features)
 
     def project(s):
         for copy in s.small_done:
@@ -430,6 +398,7 @@
             first_rows(s.x, s.small, s.weight, s.first, s.rows, step)
         write_messages(s.rows, s.mine, s.heads)
         s.sends = send_blocks(copies, at, s.mine, s.got)
+        s.writes = [copies.local(s.weight, s.weight_out), copies.local(s.first, s.first_out)]
 
     def gather_rest(s):
         pieces = (s.proj_t, s.up, s.down_t) if s.heads == 4 else (s.proj, s.up, s.down)
@@ -440,32 +409,47 @@
 
     project(image)
     text.gather.forward()
+    gather_rest(text)
+    project(text)
     gather_rest(image)
-    project(text)
-    gather_rest(text)
-    for gather in image.rest:
+    for gather in text.rest:
         gather.forward()
     for copy in image.sends:
         copy.wait()
-    image.keep = copies.local(image.got, image.messages)
-    attend_image(at, image.got, image.seg_col, image.seg_row, image.o, image.lse)
+    image.writes.append(copies.local(image.got, image.messages))
+    s = image
+    s.o[...] = jnp.zeros_like(s.o)
+    mark_keys(s.got, s.features[1], 2, s.score_keys, s.value_keys)
+    attend(
+        at, s.got, s.features[0], s.score_keys, s.value_keys, s.o, s.lse, image_task, 0, 12, 4, False
+    )
     image.o_done = send_blocks(copies, at, image.o, image.o_got)
-    for gather in text.rest:
-        gather.forward()
+    image.writes.append(copies.local(image.o, image.o_out))
+    image.rest[0].forward()
     for copy in text.sends:
         copy.wait()
-    text.keep = copies.local(text.got, text.messages)
-    attend_text(text.got, text.seg_col, text.seg_row, text.o, text.lse)
+    text.writes.append(copies.local(text.got, text.messages))
+    s = text
+    s.o[...] = jnp.zeros_like(s.o)
+    mark_keys(s.got, s.features[1], 1, s.score_keys, s.value_keys)
+    for begin, end in ((0, 4), (4, 8)):
+        attend(
+            at, s.got, s.features[0], s.score_keys, s.value_keys, s.o, s.lse, text_task,
+            begin, end, end // 2, True,
+        )
     text.o_done = send_blocks(copies, at, text.o, text.o_got)
+    text.writes.append(copies.local(text.o, text.o_out))
+    whole = [image.gather, text.gather, image.rest[0]] + text.rest
+    for gather in whole[2:]:
+        gather.arrived()
+    for gather in whole:
+        gather.sent()
+    for gather in image.rest[1:]:
+        gather.near()
     for s in (image, text):
-        for gather in s.rest:
-            gather.arrived()
-        for gather in [s.gather] + s.rest:
-            gather.sent()
         for copy in s.small_done:
             copy.wait_send()
-        s.keep.wait()
-        for copy in s.o_done:
+        for copy in s.writes + s.o_done:
             copy.wait()
 
 
@@ -486,11 +470,11 @@
             jax.ShapeDtypeStruct((width, own), BF16),
             jax.ShapeDtypeStruct((width, hidden), BF16),
             jax.ShapeDtypeStruct((width, hidden), BF16),
-            jax.ShapeDtypeStruct((4, QB if own == 4 * HD else KB, LANES), BF16),
-            jax.ShapeDtypeStruct((4 * tokens // QB, 16, QB), F32),
-            jax.ShapeDtypeStruct((4, QB if own == 4 * HD else KB, LANES), BF16),
+            jax.ShapeDtypeStruct(mixed_shape(own // HD), BF16),
+            jax.ShapeDtypeStruct((2 * (own // HD), 8, QB), F32),
+            jax.ShapeDtypeStruct(mixed_shape(own // HD), BF16),
         ]
-        out_specs += [vmem, vmem, vmem, hbm, hbm, hbm, hbm, vmem, vmem, hbm]
+        out_specs += [hbm, vmem, hbm, hbm, hbm, hbm, hbm, hbm, vmem, hbm]
         scratch += [
             pltpu.VMEM((3, 16, width), F32),
             pltpu.VMEM((16, width), F32),
@@ -501,14 +485,24 @@
             pltpu.VMEM(messages, BF16),
             pltpu.VMEM((width // 4, hidden), BF16),
             pltpu.VMEM((width // 4, own), BF16),
-            pltpu.VMEM((4 * tokens, LANES), F32),
+            pltpu.VMEM((4 * tokens, LANES), BF16),
+            pltpu.VMEM((4 * tokens, LANES), BF16),
+            pltpu.VMEM((1 if own == 4 * HD else 2, 4 * tokens, LANES), BF16),
+            pltpu.VMEM((1 if own == 4 * HD else 2, 4 * tokens, LANES), BF16),
+            pltpu.VMEM(x.shape, BF16),
+            pltpu.VMEM(up.shape, BF16),
+            pltpu.VMEM(down.shape, BF16),
+            pltpu.VMEM(proj.shape, BF16),
+            pltpu.VMEM((3, width, own), BF16),
+            pltpu.VMEM((width, tokens), BF16),
+            pltpu.VMEM(mixed_shape(own // HD), BF16),
         ]
     results = pl.pallas_call(
         front_kernel,
         out_shape=out_shape,
-        in_specs=[vmem] * (2 * FRONT_IN),
+        in_specs=[hbm, vmem, vmem, vmem, vmem, vmem, hbm, hbm, hbm] * 2,
         out_specs=out_specs,
-        scratch_shapes=scratch + copy_sems(2 * (3 + 4 * 4 + 6), 2 * 7),
+        scratch_shapes=scratch + copy_sems(2 * (3 + 4 * 4 + 6), 2 * 14),
         compiler_params=pltpu.CompilerParams(
             collective_id=0, has_side_effects=True, vmem_limit_bytes=63 << 20
         ),
@@ -692,45 +686,45 @@
     return ref[index, rows].astype(F32)
 
 
+def take_halves(got, out, at, heads, start, put):
+    half = out.shape[0] // 2
+    for tile in range(heads // 2):
+        base = 0 if tile < 2 else start
+        if tile < 2:
+            one, two = 2 * tile, 2 * tile + 1
+        else:
+            one, two = at.here_high * 2, at.here_high * 2 + 1
+        rows = slice(base, base + QB)
+        left, right = as_f32(got, one, rows), as_f32(got, two, rows)
+        for side in range(2):
+            put(tile, slice(side * half, side * half + half), lane_pair((left, side), (right, side)))
+
+
 def take_mixed(got, mixed, at, heads):
-    tokens = mixed.shape[0]
-    if heads == 4:
-        half = tokens // 2
-        for tile in range(2):
-            cols = slice(tile * LANES, (tile + 1) * LANES)
-            one, two = as_f32(got, 2 * tile), as_f32(got, 2 * tile + 1)
-            mixed[:half, cols] = lane_pair((one, 0), (two, 0)).astype(BF16)
-            mixed[half:, cols] = lane_pair((one, 1), (two, 1)).astype(BF16)
-        return
-    for tile in range(2):
-        cols = slice(tile * LANES, (tile + 1) * LANES)
-        mixed[:, cols] = lane_pair(
-            (as_f32(got, 2 * tile), 1), (as_f32(got, 2 * tile + 1), 1)
-        ).astype(BF16)
-    part = at.here // 2
-    mixed[:, 2 * LANES :] = lane_pair((as_f32(got, part), 0), (as_f32(got, part + 2), 0)).astype(BF16)
+    def put(tile, rows, value):
+        mixed[rows, tile * LANES : (tile + 1) * LANES] = value.astype(BF16)
+
+    take_halves(got, mixed, at, heads, QB, put)
 
 
 def write_grad_o(grad, out, heads):
-    tokens = grad.shape[0]
-    half = tokens // 2
     for c in range(4):
-        if heads == 4:
-            out[c] = lane_pair(
-                head_tile(grad, 0, c, slice(0, half)), head_tile(grad, 0, c, slice(half, None))
-            ).astype(BF16)
-        else:
-            out[c] = lane_pair(head_tile(grad, 0, 4 + c // 2), head_tile(grad, 0, c)).astype(BF16)
+        out[c, :QB] = halves_pair(grad, 0, c)
+        if heads == 6:
+            out[c, QB:] = halves_pair(grad, 0, 4 + c % 2)
 
 
 def send_blocks(copies, at, mine, out):
+    rows = mine.shape[1]
+    far = rows if rows in (QB, QB + KB) else rows - QB
     done = [copies.local(mine.at[at.here], out.at[at.here])]
-    for other in at.ctx[1:]:
-        done.append(copies.remote(mine.at[other], out.at[at.here], {CTX: other}))
+    for other, device, size in zip(at.ctx[1:], at.to_ctx[1:], (rows, far, far)):
+        part = pl.ds(0, size)
+        done.append(copies.remote(mine.at[other, part], out.at[at.here, part], device))
     return done
 
 
-MIDDLE_IN, MIDDLE_OUT, MIDDLE_SCRATCH = 7, 5, 17
+MIDDLE_IN, MIDDLE_OUT, MIDDLE_SCRATCH = 7, 5, 22
 
 
 def middle_kernel(*refs):
@@ -745,26 +739,49 @@
     streams = []
     for in_refs, out_refs, own in zip(ins, outs, scratch):
         s = Bag()
-        s.o, s.x, s.dy, s.small, proj_in, up_in, down_in = in_refs
-        s.y, s.dmid, s.do_out, s.rest_out, s.sums = out_refs
+        o_in, x_in, dy_in, s.small, proj_in, up_in, down_in = in_refs
+        s.y_out, s.dmid_out, s.do_out, s.rest_out, s.sums = out_refs
         (
             s.proj, s.up, s.down, s.rest, s.mixed, s.part, s.part_in, s.mid, s.first, s.first_t, s.dy_t,
-            s.act, s.dz, s.grad, s.grad_in, s.do, s.do_mine,
+            s.act, s.dz, s.grad, s.grad_in, s.do, s.do_mine, s.o, s.x, s.dy, s.y, s.dmid,
         ) = own
         s.heads = proj_in.shape[1] // HD
+        s.o_done = copies.local(o_in, s.o)
         s.proj_done = copies.local(proj_in, s.proj)
-        s.rest_done = [copies.local(up_in, s.up), copies.local(down_in, s.down)]
+        s.rows_done = [copies.local(x_in, s.x), copies.local(dy_in, s.dy)]
+        s.weights = ((up_in, s.up), (down_in, s.down))
         streams.append(s)
     text, image = streams
+    text.rest_done = [copies.local(src, dst) for src, dst in text.weights]
+    quarter = image.up.shape[0] // 4
+    near = [
+        pl.ds(pl.multiple_of(owner * quarter, 8), quarter)
+        for owner in (at.group, at.group_x, at.group_y)
+    ]
+    image.rest_done = [
+        copies.local(src.at[rows, :], dst.at[rows, :])
+        for src, dst in image.weights
+        for rows in near
+    ]
     meet([at.to_x, at.to_y] + at.to_ctx[1:] + [at.to_core])
+    top = pl.ds(pl.multiple_of(at.group_y * quarter, 8), quarter // 2)
+    low = pl.ds(pl.multiple_of(at.group_x * quarter + quarter // 2, 8), quarter // 2)
+    image.far_done = []
+    for src, dst in image.weights:
+        image.far_done.append(copies.remote(src.at[top, :], dst.at[top, :], at.to_x))
+        image.far_done.append(copies.remote(src.at[low, :], dst.at[low, :], at.to_y))
+    text.far_done = []
 
     def project(s):
+        s.o_done.wait()
         take_mixed(s.o, s.mixed, at, s.heads)
         s.proj_done.wait()
         for cols in chunks(s.x.shape[1]):
             s.part[:, cols] = dot(s.mixed[...], s.proj[cols, :], ((1,), (1,)))
         s.part_done = copies.remote(s.part, s.part_in, at.to_core)
         s.sums[...] = jnp.zeros_like(s.sums)
+        for copy in s.rows_done:
+            copy.wait()
         for rows in chunks(s.dy.shape[0]):
             s.dy_t[:, rows] = jnp.transpose(s.dy[rows, :])
 
@@ -785,6 +802,8 @@
         hidden, own = s.up.shape[1], s.proj.shape[1]
         for copy in s.rest_done:
             copy.wait()
+        for copy in s.far_done:
+            copy.wait_recv()
 
         def tile(index, carry):
             cols = pl.ds(pl.multiple_of(index * 256, 256), 256)
@@ -839,6 +858,7 @@
             low = dmid.astype(BF16)
             s.first_t[:, rows] = jnp.transpose(low)
             s.do[rows, :] = dot(low, s.proj[...])
+        s.writes = [copies.local(s.dmid, s.dmid_out)]
         write_grad_o(s.do, s.do_mine, s.heads)
         s.do_done = send_blocks(copies, at, s.do_mine, s.do_out)
         s.rest[:, : s.proj.shape[1]] = dot(s.first_t[...], s.mixed[...]).astype(BF16)
@@ -849,6 +869,7 @@
             s.y[rows, :] = (
                 s.mid[rows, :] + s.grad[1, rows, :] + s.grad_in[1, rows, :] + s.small[5:6]
             ).astype(BF16)
+        s.writes.append(copies.local(s.y, s.y_out))
 
     project(text)
     project(image)
@@ -873,8 +894,10 @@
     plane.sent()
     keep.wait()
     for s in streams:
-        for copy in s.do_done:
+        for copy in s.do_done + s.writes:
             copy.wait()
+        for copy in s.far_done:
+            copy.wait_send()
 
 
 def middle(streams):
@@ -897,7 +920,7 @@
             else jax.ShapeDtypeStruct(rest, BF16),
             jax.ShapeDtypeStruct(small.shape, F32),
         ]
-        out_specs += [vmem, vmem, hbm, vmem if summed else hbm, vmem]
+        out_specs += [hbm, hbm, hbm, vmem if summed else hbm, vmem]
         scratch += [
             pltpu.VMEM(proj.shape, BF16),
             pltpu.VMEM(up.shape, BF16),
@@ -916,13 +939,18 @@
             pltpu.VMEM((2, tokens, width), F32),
             pltpu.VMEM((tokens, own), F32),
             pltpu.VMEM(o.shape, BF16),
+            pltpu.VMEM(o.shape, BF16),
+            pltpu.VMEM((tokens, width), BF16),
+            pltpu.VMEM((tokens, width), BF16),
+            pltpu.VMEM((tokens, width), BF16),
+            pltpu.VMEM((tokens, width), F32),
         ]
     results = pl.pallas_call(
         middle_kernel,
         out_shape=out_shape,
-        in_specs=([vmem] * 4 + [hbm] * 3) * 2,
+        in_specs=([hbm] * 3 + [vmem] + [hbm] * 3) * 2,
         out_specs=out_specs,
-        scratch_shapes=scratch + arrivals + copy_sems(2 * 6 + 6, 2 * 4 + 1),
+        scratch_shapes=scratch + arrivals + copy_sems(2 * 6 + 4 + 6, 2 * (4 + 3) + 8 + 1),
         compiler_params=pltpu.CompilerParams(
             collective_id=1, has_side_effects=True, vmem_limit_bytes=64 * 1024 * 1000
         ),
@@ -932,40 +960,26 @@
 
 
 def take_dqkv(got, out, at, heads):
-    tokens, width = out.shape[0], heads * HD
-
-    def put(which, tile, rows, low, high):
+    width = heads * HD
+
+    def put(which, tile, rows, value):
         start = which * width + tile * LANES
-        out[rows, start : start + LANES] = lane_pair(low, high).astype(BF16)
-
-    every = slice(None)
-    if heads == 4:
-        half = tokens // 2
-        top, low, keys = slice(0, half), slice(half, tokens), slice(half, half + tokens)
-        for tile in range(2):
-            one, two = 2 * tile, 2 * tile + 1
-            for side, rows in ((0, top), (1, low)):
-                put(0, tile, rows, (as_f32(got, one, top), side), (as_f32(got, two, top), side))
-            for which in (1, 2):
-                side = which - 1
-                put(which, tile, every, (as_f32(got, one, keys), side), (as_f32(got, two, keys), side))
-        return
-
-    def part(position, index):
-        return got[position, index].astype(F32)
-
-    for tile in range(2):
-        one, two = 2 * tile, 2 * tile + 1
-        put(0, tile, every, (part(one, 0), 0), (part(two, 0), 0))
-        put(1, tile, every, (part(one, 1), 0), (part(two, 1), 0))
-        put(2, tile, every, (part(one, 1), 1), (part(two, 1), 1))
-    put(0, 2, every, (part(at.here_high, 0), 1), (part(at.here_high + 2, 0), 1))
-    one, two = part(0, 2) + part(1, 2), part(2, 2) + part(3, 2)
-    put(1, 2, every, (one, 1), (two, 1))
-    put(2, 2, every, (one, 0), (two, 0))
-
-
-LAST_IN, LAST_OUT, LAST_SCRATCH = 12, 4, 18
+        out[rows, start : start + LANES] = value.astype(BF16)
+
+    take_halves(got, out, at, heads, QB + 2 * KB, functools.partial(put, 0))
+
+    def keys(position, head):
+        return as_f32(got, position, key_rows(head))
+
+    pairs = [(keys(0, 0), keys(1, 0)), (keys(2, 0), keys(3, 0))]
+    if heads == 6:
+        pairs.append((keys(0, 1) + keys(2, 1), keys(1, 1) + keys(3, 1)))
+    for tile, (one, two) in enumerate(pairs):
+        put(1, tile, slice(None), lane_pair((one, 0), (two, 0)))
+        put(2, tile, slice(None), lane_pair((one, 1), (two, 1)))
+
+
+LAST_IN, LAST_OUT, LAST_SCRATCH = 12, 4, 21
 
 
 def last_kernel(*refs):
@@ -986,14 +1000,15 @@
             s.m_in, s.do_in, s.o_in, s.lse, s.seg_row, s.first_in, s.x_in, s.small, s.weight_in, s.dmid_in,
             s.rest, s.sums_in,
         ) = in_refs
-        s.grad_rows, s.sums, s.rest_final, s.qkv_final = out_refs
+        s.grad_rows_out, s.sums, s.rest_final, s.qkv_final = out_refs
         (
-            s.m, s.do, s.o, s.seg_col, s.acc, s.back, s.got, s.dqkv, s.weight, s.first, s.x, s.dmid,
+            s.m, s.do, s.o, s.query_doc, s.key_doc, s.score_keys, s.grad_rows, s.acc, s.back, s.got, s.dqkv, s.weight, s.first, s.x, s.dmid,
             s.part, s.part_in, s.g_qkv, s.sums_own, s.sums_out, s.sums_got,
         ) = own[:LAST_SCRATCH]
         s.rest_line, s.qkv_line = own[LAST_SCRATCH : LAST_SCRATCH + 3], own[LAST_SCRATCH + 3 : LAST_SCRATCH + 6]
         s.qkv_arrivals = own[LAST_SCRATCH + 6 :]
         s.heads = s.weight.shape[2] // HD
+        s.features = (s.query_doc, s.key_doc)
         s.reads = [
             copies.local(src, dst) for src, dst in ((s.m_in, s.m), (s.do_in, s.do), (s.o_in, s.o))
         ]
@@ -1011,7 +1026,7 @@
     )
     text_line.gather()
     for s in (image, text):
-        document_columns(s.seg_row, s.seg_col)
+        document_features(s.seg_row, *s.features)
     for s in streams:
         s.loads = [
             copies.local(src, dst)
@@ -1019,28 +1034,30 @@
                 (s.weight_in, s.weight), (s.first_in, s.first), (s.x_in, s.x), (s.dmid_in, s.dmid),
             )
         ]
-    image.acc[...] = jnp.zeros_like(image.acc)
-    image.back[...] = jnp.zeros_like(image.back)
     for s in (image, text):
         for copy in s.reads:
             copy.wait()
-
-    def image_tasks(begin, end):
-        s = image
-        unattend_image(at, s.m, s.do, s.o, s.lse, s.seg_col, s.seg_row, s.acc, s.back, begin, end)
-
-    image_tasks(0, 6)
+    for s in (image, text):
+        s.acc[...] = jnp.zeros_like(s.acc)
+        s.back[...] = jnp.zeros_like(s.back)
+        mark_keys(s.m, s.features[1], s.acc.shape[0], s.score_keys, None)
+
+    def unattend_tasks(s, *task):
+        unattend(
+            at, s.m, s.do, s.o, s.lse, s.features[0], s.score_keys, s.acc, s.back, *task
+        )
+
+    unattend_tasks(image, image_task, 0, 8, 4, False)
     text_line.join()
-    image_tasks(6, 12)
-    for source in range(4):
-        image.back[source, 1] = image.acc[0, key_range(source)].astype(BF16)
-        image.back[source, 2] = image.acc[1, key_range(source)].astype(BF16)
+    unattend_tasks(image, image_task, 8, 12, 4, False)
+    key_gradients(image.acc, image.back)
     image.sends = send_blocks(copies, at, image.back, image.got)
-    text_line.share()
-    s = text
-    unattend_text(s.m, s.do, s.o, s.lse, s.seg_col, s.seg_row, s.acc.at[0], s.back)
+    unattend_tasks(text, text_task, 0, 4, 2, True)
+    unattend_tasks(text, text_task, 4, 8, 4, True)
+    key_gradients(text.acc, text.back)
     text.sends = send_blocks(copies, at, text.back, text.got)
     plane.cross()
+    text_line.share()
 
     def project(s):
         width = s.x.shape[1]
@@ -1079,6 +1096,7 @@
             )
             s.sums_own[0:1] += jnp.sum(first * normed, axis=0, keepdims=True)
             s.sums_own[2:3] += jnp.sum(first, axis=0, keepdims=True)
+        s.write = copies.local(s.grad_rows, s.grad_rows_out)
         s.sums_done = [copies.remote(s.sums_own, s.sums_got.at[0], at.to_x)]
 
     def add_sums(s, step):
@@ -1090,38 +1108,40 @@
             device = (at.to_y, at.to_ctx[1], at.to_ctx[2])[step]
             s.sums_done.append(copies.remote(after, s.sums_got.at[step + 1], device))
 
-    project(image)
     plane.arrived()
-    middle_column = plane.columns // (2 * STEP) * STEP
+    third = plane.columns // (3 * STEP) * STEP
     rest_lines = [
         LineSum(copies, at, plane.halves, image.rest_line, image.rest_final, begin, end)
-        for begin, end in ((0, middle_column), (middle_column, plane.columns))
+        for begin, end in ((0, third), (third, 2 * third), (2 * third, plane.columns))
     ]
-    rest_lines[0].gather()
+    for line in rest_lines:
+        line.gather()
+    project(image)
+    rest_lines[0].join()
     input_grad(image)
     image.qkv_plane.cross()
-    rest_lines[1].gather()
+    rest_lines[1].join()
     project(text)
-    rest_lines[0].join()
+    rest_lines[0].share()
+    image.qkv_plane.arrived()
+    image.qkv_sum.gather()
+    rest_lines[2].join()
     input_grad(text)
     text.qkv_plane.cross()
-    image.qkv_plane.arrived()
-    image.qkv_sum.gather()
-    rest_lines[1].join()
-    add_sums(image, 0)
-    rest_lines[0].share()
-    add_sums(text, 0)
+    rest_lines[1].share()
+    image.qkv_sum.join()
     text.qkv_plane.arrived()
     text.qkv_sum.gather()
-    image.qkv_sum.join()
+    add_sums(image, 0)
+    add_sums(text, 0)
+    rest_lines[2].share()
+    text.qkv_sum.join()
     add_sums(image, 1)
     add_sums(text, 1)
-    rest_lines[1].share()
-    text.qkv_sum.join()
+    image.qkv_sum.share()
+    text.qkv_sum.share()
     add_sums(image, 2)
     add_sums(text, 2)
-    image.qkv_sum.share()
-    text.qkv_sum.share()
     add_sums(image, 3)
     add_sums(text, 3)
     for line in [text_line] + rest_lines + [image.qkv_sum, text.qkv_sum]:
@@ -1131,6 +1151,7 @@
         s.qkv_plane.sent()
         for copy in s.sums_done:
             copy.wait_send()
+        s.write.wait()
 
 
 def last(streams):
@@ -1150,7 +1171,10 @@
             pltpu.VMEM(messages.shape, BF16),
             pltpu.VMEM(do.shape, BF16),
             pltpu.VMEM(do.shape, BF16),
-            pltpu.VMEM((4 * tokens, LANES), F32),
+            pltpu.VMEM((4 * tokens, LANES), BF16),
+            pltpu.VMEM((4 * tokens, LANES), BF16),
+            pltpu.VMEM((1 if own == 4 * HD else 2, 4 * tokens, LANES), BF16),
+            pltpu.VMEM((tokens, width), F32),
             pltpu.VMEM((1 if own == 4 * HD else 2, 4 * tokens, LANES), F32),
             pltpu.VMEM(messages.shape, BF16),
             pltpu.VMEM(messages.shape, BF16),
@@ -1175,8 +1199,8 @@
         last_kernel,
         out_shape=out_shape,
         in_specs=specs,
-        out_specs=[vmem] * 8,
-        scratch_shapes=scratch + copy_sems(2 * (3 + 1 + 4 + 6) + 6 + 3 * 5, 2 * (1 + 7) + 3),
+        out_specs=[hbm, vmem, vmem, vmem] * 2,
+        scratch_shapes=scratch + copy_sems(2 * (3 + 1 + 4 + 6) + 6 + 3 * 6, 2 * (1 + 7 + 1) + 3),
         compiler_params=pltpu.CompilerParams(
             collective_id=2, has_side_effects=True, vmem_limit_bytes=64 * 1024 * 1000
         ),

time: 322 us -> 284 us (0.88); the launches traced: 318 us -> 284 us
  Pallas kernels: 313 us -> 279 us
    pallas_call x1, Pallas kernels: 161 us -> 137 us  [last(): pl.pallas_call(last_kernel, out_shape=out_shape, in_specs=specs, out_spec...]
    pallas_call x2, Pallas kernels: 148 us -> 138 us  [the longest x1 97.3 us: front(): pl.pallas_call(front_kernel, out_shape=out_shape, in_specs=[hbm, vmem, vm...]
where the time goes in v1:
time: 284 us
  Pallas kernels  279 us (98%)
  local copies, waits for them, and re-layouts  4.03 us (1%)
    pallas_call x1, Pallas kernels, last(): pl.pallas_call(last_kernel, out_shape=out_shape, in_specs=specs, out_spec...  137 us
    pallas_call x1, Pallas kernels, front(): pl.pallas_call(front_kernel, out_shape=out_shape, in_specs=[hbm, vmem, vm...  97.3 us
    pallas_call x1, Pallas kernels, middle(): pl.pallas_call(middle_kernel, out_shape=out_shape, in_specs=([hbm] * 3 +...  40.2 us

profile of v1, /device:TPU:0, one launch (start us, length us, event | category | flops | bytes accessed | tf_op | source)
XLA Modules:
  0.0 283.9 jit_solution(1996296247998261709)
XLA Ops:
  0.7 97.3 %front.1 = (bf16[3,512,256]{2,1,0:T(8,128)(2,1)}, f32[16,512]{1,0:T(8,128)}, bf16[512,512]{1,0:T(8,128)(2,1)}, bf16[4,768,128]{2,1,0:T(8,128)(2,1)}, bf16[512,25...) custom-call(bf16[512,512]{1,0:T(8,128)(2,1)} %bitcast.15, ...), custom_call_target="tpu_custom_call" | custom-call | tf_op jit(solution)/shard_map/front/pallas_call | solution.py:500
  98.0 40.2 %middle.1 = (bf16[512,512]{1,0:T(8,128)(2,1)}, f32[512,512]{1,0:T(8,128)}, bf16[4,256,128]{2,1,0:T(8,128)(2,1)}, f32[128,2304]{1,0:T(8,128)}, f32[16,512]{1,0:T(...) custom-call(bf16[4,256,128]{2,1,0:T(8,128)(2,1)} %get-tuple-element., ...), custom_call_target="tpu_custom_call" | custom-call | tf_op jit(solution)/shard_map/middle/pallas_call | solution.py:948
  138.2 137.3 %last.1 = (f32[512,512]{1,0:T(8,128)}, f32[16,512]{1,0:T(8,128)}, bf16[128,2304]{1,0:T(8,128)(2,1)}, bf16[128,768]{1,0:T(8,128)(2,1)}, f32[512,768]{1,0:T(8,128)...) custom-call(bf16[4,768,128]{2,1,0:T(8,128)(2,1)} %get-tuple-element.81.refs_0_, ...), custom_call_target="tpu_custom_call" | custom-call | tf_op jit(solution)/shard_map/last/pallas_call | solution.py:1198
  275.5 0.0 copy-start.2
  275.5 0.0 copy-start
  275.5 4.4 %finish.1 = (f32[2,128]{1,0:T(2,128)}, f32[4,128]{1,0:T(4,128)}, f32[1,384]{1,0:T(1,128)}, f32[3,128,256]{2,1,0:T(8,128)}, f32[256,128]{1,0:T(8,128)}, /*index=5...) custom-call(f32[16,512]{1,0:T(8,128)} %get-tuple-element.100.refs_0_, ...), custom_call_target="tpu_custom_call" | custom-call | tf_op jit(solution)/shard_map/finish/pallas_call | solution.py:1250
  279.9 0.0 copy-done.2
  279.9 0.9 copy.42
  280.8 0.0 copy-done
  280.8 0.0 copy-start.3
  280.8 0.0 copy-start.1
  280.8 1.1 copy.43
  281.9 0.2 copy-done.3
  282.2 0.8 copy.44
  283.0 0.0 copy-done.1
  283.0 1.0 copy.45
Async XLA Ops:
  275.5 4.4 %copy-start.2 = (bf16[512,768]{1,0:T(8,128)(2,1)S(1)}, bf16[512,768]{1,0:T(8,128)(2,1)}, u32[]{:S(2)}) copy-start(bf16[512,768]{1,0:T(8,128)(2,1)} %get-tuple-element.80) | copy-start | bytes 2359300
  275.5 5.3 %copy-start = (f32[512,768]{1,0:T(8,128)S(1)}, f32[512,768]{1,0:T(8,128)}, u32[]{:S(2)}) copy-start(f32[512,768]{1,0:T(8,128)} %get-tuple-element.99) | copy-start | bytes 4718596
  280.8 1.4 copy-start.3
  280.8 2.2 copy-start.1

commit v2 on v1

--- a/solution.py
+++ b/solution.py
@@ -94,7 +94,9 @@
 
 def image_task(at, task):
     shared = 1 - (task + 8) // 12
-    return shared, pick(shared, at.here_high * 2 + task // 2, task // 2 - 2), task % 2
+    step = 5 - task // 2
+    low, high = (at.here_low + step % 2) % 2, (at.here_high + step // 2) % 2
+    return shared, pick(shared, at.here_high * 2 + task // 2, high * 2 + low), task % 2
 
 
 def attend(at, m, features, score_keys, value_keys, o, lse, task_of, begin, end, blocks, causal):
@@ -155,10 +157,9 @@
     lax.fori_loop(begin, end, one, 0)
 
 
-def key_gradients(acc, out):
-    for head in range(acc.shape[0]):
-        for index in range(4):
-            out[index, key_rows(head)] = acc[head, key_range(index)].astype(BF16)
+def key_gradients(acc, out, head):
+    for index in range(4):
+        out[index, key_rows(head)] = acc[head, key_range(index)].astype(BF16)
 
 
 class Bag:
@@ -168,7 +169,7 @@
 def partners():
     at = Bag()
     group, here, core = lax.axis_index(FSDP), lax.axis_index(CTX), lax.axis_index(TP)
-    at.group, at.here = group, here
+    at.group, at.here, at.core = group, here, core
     at.group_x = group + 1 - 2 * (group % 2)
     at.group_y = group + 2 - 4 * (group // 2)
     at.group_far = 3 - group
@@ -181,11 +182,14 @@
     return at
 
 
-def meet(devices):
+def greet(devices):
     barrier = pltpu.get_barrier_semaphore()
     for device in devices:
         pl.semaphore_signal(barrier, inc=1, device_id=device, device_id_type=MESH)
-    pl.semaphore_wait(barrier, len(devices))
+
+
+def meet(devices):
+    pl.semaphore_wait(pltpu.get_barrier_semaphore(), len(devices))
 
 
 class Copies:
@@ -208,11 +212,12 @@
             copy.start()
         return copy
 
-    def local(self, src, dst):
+    def local(self, src, dst, start=True):
         index = self.used[1]
         self.used[1] += 1
         copy = pltpu.make_async_copy(src, dst, self.sems[2].at[index])
-        copy.start()
+        if start:
+            copy.start()
         return copy
 
 
@@ -347,6 +352,8 @@
     refs = refs[2 * FRONT_OUT :]
     scratch = [refs[:FRONT_SCRATCH], refs[FRONT_SCRATCH : 2 * FRONT_SCRATCH]]
     copies = Copies(*refs[2 * FRONT_SCRATCH :])
+    others = [at.to_x, at.to_y, at.to_far] + at.to_ctx[1:]
+    greet(others)
     streams = []
     for in_refs, out_refs, own in zip(ins, outs, scratch):
         s = Bag()
@@ -369,25 +376,23 @@
             )
         ]
         streams.append(s)
-    meet([at.to_x, at.to_y, at.to_far] + at.to_ctx[1:])
     text, image = streams
-    image.gather = Gather(copies, at, image.qkv, image.weight)
     for s in (image, text):
         spread_small(at, s.gains, s.shifts, s.bias, s.wide, s.flat, s.small_own)
-    for s in (image, text):
+        document_features(s.seg_row, *s.features)
+    meet(others)
+    text.gather = Gather(copies, at, text.qkv, text.weight)
+    for s in (text, image):
         s.small_done = [
             copies.remote(s.small_own, s.small_in.at[i], device)
             for i, device in enumerate((at.to_x, at.to_y, at.to_far))
         ]
-    image.gather.forward()
-    text.gather = Gather(copies, at, text.qkv, text.weight)
-    for s in (image, text):
         for copy in s.reads:
             copy.wait()
     text.down_t[...] = jnp.transpose(text.down[...])
     text.proj_t[...] = jnp.transpose(text.proj[...])
-    for s in (image, text):
-        document_features(s.seg_row, *s.features)
+    text.gather.forward()
+    image.gather = Gather(copies, at, image.qkv, image.weight)
 
     def project(s):
         for copy in s.small_done:
@@ -397,7 +402,6 @@
         for step in range(s.x.shape[0] // 256):
             first_rows(s.x, s.small, s.weight, s.first, s.rows, step)
         write_messages(s.rows, s.mine, s.heads)
-        s.sends = send_blocks(copies, at, s.mine, s.got)
         s.writes = [copies.local(s.weight, s.weight_out), copies.local(s.first, s.first_out)]
 
     def gather_rest(s):
@@ -407,38 +411,50 @@
             for piece, full in zip(pieces, (s.proj_full, s.up_full, s.down_full))
         ]
 
+    project(text)
+    text.sends = send_blocks(copies, at, text.mine, text.got)
+    image.gather.forward()
+    gather_rest(text)
     project(image)
-    text.gather.forward()
-    gather_rest(text)
-    project(text)
+    image.sends = send_blocks(copies, at, image.mine, image.got)
     gather_rest(image)
-    for gather in text.rest:
+    s = text
+    for copy in s.sends:
+        copy.wait()
+    s.writes.append(copies.local(s.got, s.messages))
+    s.o[...] = jnp.zeros_like(s.o)
+    mark_keys(s.got, s.features[1], 1, s.score_keys, s.value_keys)
+    attend(
+        at, s.got, s.features[0], s.score_keys, s.value_keys, s.o, s.lse, text_task, 0, 8, 4, True
+    )
+    for gather in s.rest:
         gather.forward()
-    for copy in image.sends:
+    s = image
+    for copy in s.sends:
         copy.wait()
-    image.writes.append(copies.local(image.got, image.messages))
-    s = image
+    text.o_done = send_blocks(copies, at, text.o, text.o_got)
+    s.writes.append(copies.local(s.got, s.messages))
     s.o[...] = jnp.zeros_like(s.o)
     mark_keys(s.got, s.features[1], 2, s.score_keys, s.value_keys)
-    attend(
-        at, s.got, s.features[0], s.score_keys, s.value_keys, s.o, s.lse, image_task, 0, 12, 4, False
-    )
-    image.o_done = send_blocks(copies, at, image.o, image.o_got)
-    image.writes.append(copies.local(image.o, image.o_out))
-    image.rest[0].forward()
-    for copy in text.sends:
-        copy.wait()
-    text.writes.append(copies.local(text.got, text.messages))
-    s = text
-    s.o[...] = jnp.zeros_like(s.o)
-    mark_keys(s.got, s.features[1], 1, s.score_keys, s.value_keys)
-    for begin, end in ((0, 4), (4, 8)):
+    s.o_done = send_blocks(copies, at, s.o, s.o_got, start=False)
+
+    def image_pair(index, carry):
         attend(
-            at, s.got, s.features[0], s.score_keys, s.value_keys, s.o, s.lse, text_task,
-            begin, end, end // 2, True,
+            at, image.got, image.features[0], image.score_keys, image.value_keys, image.o, image.lse,
+            image_task, 2 * index, 2 * index + 2, 4, False,
         )
-    text.o_done = send_blocks(copies, at, text.o, text.o_got)
-    text.writes.append(copies.local(text.o, text.o_out))
+        for step, copy in enumerate(image.o_done):
+
+            @pl.when(index == 5 - step)
+            def _(copy=copy):
+                copy.start()
+
+        return carry
+
+    lax.fori_loop(0, 6, image_pair, 0)
+    s.rest[0].forward()
+    for s in (text, image):
+        s.writes.append(copies.local(s.o, s.o_out))
     whole = [image.gather, text.gather, image.rest[0]] + text.rest
     for gather in whole[2:]:
         gather.arrived()
@@ -512,6 +528,7 @@
 
 
 STEP = 384
+TILES = 1
 
 
 def by_columns(columns, body):
@@ -545,6 +562,10 @@
         else:
             self.loads = [copies.local(part, load) for part, load in zip(parts, loads)]
             self.pass_top, self.pass_low, self.own = loads
+        self.second = [
+            copies.remote(self.pass_top, self.in_top, at.to_y, False),
+            copies.remote(self.pass_low, self.in_low, at.to_x, False),
+        ]
 
     def cross(self):
         for copy in self.loads:
@@ -557,7 +578,7 @@
             ).astype(BF16)
 
         by_columns(self.columns, top)
-        self.second = [self.copies.remote(self.pass_top, self.in_top, self.at.to_y)]
+        self.second[0].start()
         self.first[1].wait_recv()
 
         def low(cols):
@@ -566,7 +587,7 @@
             ).astype(BF16)
 
         by_columns(self.columns, low)
-        self.second.append(self.copies.remote(self.pass_low, self.in_low, self.at.to_x))
+        self.second[1].start()
 
     def arrived(self):
         for copy in self.first[2:] + self.second:
@@ -714,13 +735,15 @@
             out[c, QB:] = halves_pair(grad, 0, 4 + c % 2)
 
 
-def send_blocks(copies, at, mine, out):
+def send_blocks(copies, at, mine, out, begin=0, end=None, start=True):
     rows = mine.shape[1]
-    far = rows if rows in (QB, QB + KB) else rows - QB
-    done = [copies.local(mine.at[at.here], out.at[at.here])]
-    for other, device, size in zip(at.ctx[1:], at.to_ctx[1:], (rows, far, far)):
-        part = pl.ds(0, size)
-        done.append(copies.remote(mine.at[other, part], out.at[at.here, part], device))
+    end = rows if end is None else end
+    far = min(end, rows if rows in (QB, QB + KB) else rows - QB)
+    part = pl.ds(begin, end - begin)
+    done = [copies.local(mine.at[at.here, part], out.at[at.here, part], start)]
+    for other, device, last in zip(at.ctx[1:], at.to_ctx[1:], (end, far, far)):
+        part = pl.ds(begin, last - begin)
+        done.append(copies.remote(mine.at[other, part], out.at[at.here, part], device, start))
     return done
 
 
@@ -736,6 +759,8 @@
     scratch = [refs[:MIDDLE_SCRATCH], refs[MIDDLE_SCRATCH : 2 * MIDDLE_SCRATCH]]
     arrivals = refs[2 * MIDDLE_SCRATCH : 2 * MIDDLE_SCRATCH + 4]
     copies = Copies(*refs[2 * MIDDLE_SCRATCH + 4 :])
+    others = [at.to_x, at.to_y] + at.to_ctx[1:] + [at.to_core]
+    greet(others)
     streams = []
     for in_refs, out_refs, own in zip(ins, outs, scratch):
         s = Bag()
@@ -763,7 +788,7 @@
         for src, dst in image.weights
         for rows in near
     ]
-    meet([at.to_x, at.to_y] + at.to_ctx[1:] + [at.to_core])
+    meet(others)
     top = pl.ds(pl.multiple_of(at.group_y * quarter, 8), quarter // 2)
     low = pl.ds(pl.multiple_of(at.group_x * quarter + quarter // 2, 8), quarter // 2)
     image.far_done = []
@@ -800,21 +825,21 @@
     def feed_forward(s):
         tokens, width = s.x.shape
         hidden, own = s.up.shape[1], s.proj.shape[1]
+        size = width // TILES
         for copy in s.rest_done:
             copy.wait()
         for copy in s.far_done:
             copy.wait_recv()
 
         def tile(index, carry):
-            cols = pl.ds(pl.multiple_of(index * 256, 256), 256)
+            cols = pl.ds(pl.multiple_of(index * size, LANES), size)
             up, down = s.up[:, cols], s.down[:, cols]
-            per_row = width // 256
-            up_cols = pl.ds(pl.multiple_of(own + index * 256, LANES), 256)
-            down_cols = pl.ds(pl.multiple_of(own + hidden + index * 256, LANES), 256)
-            row = pl.ds(7 + index // per_row, 1)
-            place = pl.ds(pl.multiple_of((index % per_row) * 256, 256), 256)
+            up_cols = pl.ds(pl.multiple_of(own + index * size, LANES), size)
+            down_cols = pl.ds(pl.multiple_of(own + hidden + index * size, LANES), size)
+            row = pl.ds(7 + index // (width // size), 1)
+            place = pl.ds(pl.multiple_of((index % (width // size)) * size, LANES), size)
             bias = s.small[row, place]
-            total = jnp.zeros((1, 256), F32)
+            total = jnp.zeros((1, size), F32)
             for rows in chunks(tokens):
                 z = dot(s.first[rows, :], up) + bias
                 sg = jax.nn.sigmoid(1.702 * z)
@@ -829,7 +854,7 @@
             s.rest[:, down_cols] = dot(s.dy_t[...], s.act[:, cols]).astype(BF16)
             return carry
 
-        lax.fori_loop(0, hidden // 256, tile, 0)
+        lax.fori_loop(0, hidden // size, tile, 0)
         for cols in chunks(width):
             s.grad[0, :, cols] = dot(s.dz[...], s.up[cols, :], ((1,), (1,)))
         s.grad_done = copies.remote(s.grad.at[0], s.grad_in.at[0], at.to_core)
@@ -861,6 +886,8 @@
         s.writes = [copies.local(s.dmid, s.dmid_out)]
         write_grad_o(s.do, s.do_mine, s.heads)
         s.do_done = send_blocks(copies, at, s.do_mine, s.do_out)
+
+    def proj_grad(s):
         s.rest[:, : s.proj.shape[1]] = dot(s.first_t[...], s.mixed[...]).astype(BF16)
 
     def output(s):
@@ -877,11 +904,13 @@
     feed_forward(text)
     second_norm(image)
     back(text)
+    proj_grad(text)
     plane = PlaneSum(copies, at, text.rest, arrivals)
     feed_forward(image)
     back(image)
+    plane.cross()
+    proj_grad(image)
     keep = copies.local(image.rest, image.rest_out)
-    plane.cross()
     output(text)
     output(image)
     plane.arrived()
@@ -979,7 +1008,7 @@
         put(2, tile, slice(None), lane_pair((one, 1), (two, 1)))
 
 
-LAST_IN, LAST_OUT, LAST_SCRATCH = 12, 4, 21
+LAST_IN, LAST_OUT, LAST_SCRATCH = 12, 4, 22
 
 
 def last_kernel(*refs):
@@ -993,6 +1022,8 @@
     refs = refs[2 * count :]
     rest_arrivals, rest_loads = refs[:4], refs[4:7]
     copies = Copies(*refs[7:])
+    others = [at.to_x, at.to_y] + at.to_ctx[1:] + [at.to_core]
+    greet(others)
     streams = []
     for in_refs, out_refs, own in zip(ins, outs, scratch):
         s = Bag()
@@ -1003,7 +1034,7 @@
         s.grad_rows_out, s.sums, s.rest_final, s.qkv_final = out_refs
         (
             s.m, s.do, s.o, s.query_doc, s.key_doc, s.score_keys, s.grad_rows, s.acc, s.back, s.got, s.dqkv, s.weight, s.first, s.x, s.dmid,
-            s.part, s.part_in, s.g_qkv, s.sums_own, s.sums_out, s.sums_got,
+            s.part, s.part_in, s.g_qkv, s.sums_own, s.sums_out, s.sums_got, s.sums_line,
         ) = own[:LAST_SCRATCH]
         s.rest_line, s.qkv_line = own[LAST_SCRATCH : LAST_SCRATCH + 3], own[LAST_SCRATCH + 3 : LAST_SCRATCH + 6]
         s.qkv_arrivals = own[LAST_SCRATCH + 6 :]
@@ -1014,7 +1045,11 @@
         ]
         streams.append(s)
     text, image = streams
-    meet([at.to_x, at.to_y] + at.to_ctx[1:] + [at.to_core])
+    for s in streams:
+        document_features(s.seg_row, *s.features)
+        s.acc[...] = jnp.zeros_like(s.acc)
+        s.back[...] = jnp.zeros_like(s.back)
+    meet(others)
     plane = PlaneSum(copies, at, image.rest, rest_arrivals, rest_loads)
     text_half = text.rest.shape[0] // 2
 
@@ -1026,20 +1061,14 @@
     )
     text_line.gather()
     for s in (image, text):
-        document_features(s.seg_row, *s.features)
-    for s in streams:
+        for copy in s.reads:
+            copy.wait()
         s.loads = [
             copies.local(src, dst)
             for src, dst in (
-                (s.weight_in, s.weight), (s.first_in, s.first), (s.x_in, s.x), (s.dmid_in, s.dmid),
+                (s.first_in, s.first), (s.weight_in, s.weight), (s.x_in, s.x), (s.dmid_in, s.dmid),
             )
         ]
-    for s in (image, text):
-        for copy in s.reads:
-            copy.wait()
-    for s in (image, text):
-        s.acc[...] = jnp.zeros_like(s.acc)
-        s.back[...] = jnp.zeros_like(s.back)
         mark_keys(s.m, s.features[1], s.acc.shape[0], s.score_keys, None)
 
     def unattend_tasks(s, *task):
@@ -1047,17 +1076,35 @@
             at, s.m, s.do, s.o, s.lse, s.features[0], s.score_keys, s.acc, s.back, *task
         )
 
-    unattend_tasks(image, image_task, 0, 8, 4, False)
-    text_line.join()
-    unattend_tasks(image, image_task, 8, 12, 4, False)
-    key_gradients(image.acc, image.back)
-    image.sends = send_blocks(copies, at, image.back, image.got)
-    unattend_tasks(text, text_task, 0, 4, 2, True)
-    unattend_tasks(text, text_task, 4, 8, 4, True)
-    key_gradients(text.acc, text.back)
-    text.sends = send_blocks(copies, at, text.back, text.got)
-    plane.cross()
-    text_line.share()
+    text.sends = send_blocks(copies, at, text.back, text.got, start=False)
+    split = QB + KB
+    shared_sends = send_blocks(copies, at, image.back, image.got, split, None, False)
+    own_sends = send_blocks(copies, at, image.back, image.got, 0, split, False)
+    image.sends = shared_sends + own_sends
+
+    def image_phase(phase, carry):
+        unattend_tasks(image, image_task, phase * 4, phase * 4 + 4, 4, False)
+
+        @pl.when(phase == 0)
+        def _():
+            key_gradients(image.acc, image.back, 1)
+            for copy in shared_sends:
+                copy.start()
+            unattend_tasks(text, text_task, 0, 8, 4, True)
+            key_gradients(text.acc, text.back, 0)
+            for copy in text.sends:
+                copy.start()
+
+        @pl.when(phase == 1)
+        def _():
+            plane.cross()
+
+        return carry
+
+    lax.fori_loop(0, 3, image_phase, 0)
+    key_gradients(image.acc, image.back, 0)
+    for copy in own_sends:
+        copy.start()
 
     def project(s):
         width = s.x.shape[1]
@@ -1079,9 +1126,11 @@
         s.sums_own[...] = s.sums_in[...]
         s.sums_own[6:7, :own] = jnp.sum(s.dqkv[:, :own].astype(F32), axis=0, keepdims=True)
         s.sums_own[6:7, own:] = jnp.sum(s.dqkv[:, 2 * own :].astype(F32), axis=0, keepdims=True)
-        s.qkv_sum = LineSum(
-            copies, at, s.qkv_plane.halves, s.qkv_line, s.qkv_final, 0, 3 * own
-        )
+        cuts = (0, 3 * own) if own < STEP else (0, 2 * own, 3 * own)
+        s.qkv_sums = [
+            LineSum(copies, at, s.qkv_plane.halves, s.qkv_line, s.qkv_final, begin, end)
+            for begin, end in zip(cuts, cuts[1:])
+        ]
 
     def input_grad(s):
         s.part_done.wait()
@@ -1101,50 +1150,72 @@
 
     def add_sums(s, step):
         s.sums_done[-1].wait_recv()
-        before = s.sums_own if step == 0 else s.sums_out.at[step - 1]
-        after = s.sums if step == 3 else s.sums_out.at[step]
-        after[...] = before[...] + s.sums_got[step]
-        if step < 3:
-            device = (at.to_y, at.to_ctx[1], at.to_ctx[2])[step]
-            s.sums_done.append(copies.remote(after, s.sums_got.at[step + 1], device))
-
-    plane.arrived()
-    third = plane.columns // (3 * STEP) * STEP
+        before = s.sums_own if step == 0 else s.sums_out
+        total = before[...] + s.sums_got[step]
+        if step == 0:
+            s.sums_out[...] = total
+            s.sums_done.append(copies.remote(s.sums_out, s.sums_got.at[1], at.to_y))
+        else:
+            s.sums_line[at.here] = total
+            mine = s.sums_line.at[at.here]
+            s.sums_done += [copies.remote(mine, mine, device) for device in at.to_ctx[1:]]
+
+    def end_sums(s):
+        for copy in s.sums_done[2:]:
+            copy.wait_recv()
+        s.sums[...] = s.sums_line[0] + s.sums_line[1] + s.sums_line[2] + s.sums_line[3]
+
+    cuts = [0, STEP, 4 * STEP, 7 * STEP, plane.columns]
     rest_lines = [
         LineSum(copies, at, plane.halves, image.rest_line, image.rest_final, begin, end)
-        for begin, end in ((0, third), (third, 2 * third), (2 * third, plane.columns))
+        for begin, end in zip(cuts, cuts[1:])
     ]
+
+    def by_core(one, two):
+        @pl.when(at.core == 0)
+        def _():
+            one()
+            two()
+
+        @pl.when(at.core == 1)
+        def _():
+            two()
+            one()
+
+    project(text)
+    plane.arrived()
+    text.qkv_plane.cross()
+    input_grad(text)
     for line in rest_lines:
         line.gather()
+    text.qkv_plane.arrived()
+    text.qkv_sums[0].gather()
+    add_sums(text, 0)
     project(image)
-    rest_lines[0].join()
+    by_core(rest_lines[0].join, text_line.join)
     input_grad(image)
+    rest_lines[1].join()
     image.qkv_plane.cross()
-    rest_lines[1].join()
-    project(text)
-    rest_lines[0].share()
+    add_sums(text, 1)
+    add_sums(image, 0)
+    by_core(rest_lines[0].share, text_line.share)
+    rest_lines[2].join()
     image.qkv_plane.arrived()
-    image.qkv_sum.gather()
-    rest_lines[2].join()
-    input_grad(text)
-    text.qkv_plane.cross()
+    for line in image.qkv_sums:
+        line.gather()
+    add_sums(image, 1)
     rest_lines[1].share()
-    image.qkv_sum.join()
-    text.qkv_plane.arrived()
-    text.qkv_sum.gather()
-    add_sums(image, 0)
-    add_sums(text, 0)
+    rest_lines[3].join()
+    image.qkv_sums[0].join()
     rest_lines[2].share()
-    text.qkv_sum.join()
-    add_sums(image, 1)
-    add_sums(text, 1)
-    image.qkv_sum.share()
-    text.qkv_sum.share()
-    add_sums(image, 2)
-    add_sums(text, 2)
-    add_sums(image, 3)
-    add_sums(text, 3)
-    for line in [text_line] + rest_lines + [image.qkv_sum, text.qkv_sum]:
+    image.qkv_sums[1].join()
+    text.qkv_sums[0].join()
+    rest_lines[3].share()
+    for line in image.qkv_sums + text.qkv_sums:
+        line.share()
+    for s in streams:
+        end_sums(s)
+    for line in [text_line] + rest_lines + image.qkv_sums + text.qkv_sums:
         line.finish()
     plane.sent()
     for s in streams:
@@ -1187,7 +1258,8 @@
             pltpu.VMEM((tokens, width), F32),
             pltpu.VMEM((width, 3 * own), BF16),
             pltpu.VMEM(small.shape, F32),
-            pltpu.VMEM((3,) + small.shape, F32),
+            pltpu.VMEM(small.shape, F32),
+            pltpu.VMEM((2,) + small.shape, F32),
             pltpu.VMEM((4,) + small.shape, F32),
         ]
         scratch += LineSum.scratch(*rest_shape) + LineSum.scratch(*qkv_shape)
@@ -1200,7 +1272,7 @@
         out_shape=out_shape,
         in_specs=specs,
         out_specs=[hbm, vmem, vmem, vmem] * 2,
-        scratch_shapes=scratch + copy_sems(2 * (3 + 1 + 4 + 6) + 6 + 3 * 6, 2 * (1 + 7 + 1) + 3),
+        scratch_shapes=scratch + copy_sems(2 * (3 + 1 + 5 + 6) + 3 + 6 + 3 * 8, 2 * (1 + 7 + 1) + 3 + 1),
         compiler_params=pltpu.CompilerParams(
             collective_id=2, has_side_effects=True, vmem_limit_bytes=64 * 1024 * 1000
         ),
@@ -1215,9 +1287,22 @@
 
 
 def finish_kernel(*refs):
-    ins = [refs[:3], refs[3:6]]
-    outs = [refs[6:13], refs[13:]]
-    for (sums, rest, qkv), (gains, shifts, bias, qkv_out, proj, up, down) in zip(ins, outs):
+    ins = [refs[:5], refs[5:10]]
+    outs = [refs[10:19], refs[19:28]]
+    buffers, reads, writes = [refs[28:30], refs[30:32]], refs[32], refs[33]
+    passes = []
+    for index, (in_refs, out_refs, own) in enumerate(zip(ins, outs, buffers)):
+        for place in range(2):
+            step = 2 * index + place
+            copy = pltpu.make_async_copy(in_refs[3 + place], own[place], reads.at[step])
+            copy.start()
+            passes.append(
+                (copy, pltpu.make_async_copy(own[place], out_refs[7 + place], writes.at[step]))
+            )
+    for copy, write in passes:
+        copy.wait()
+        write.start()
+    for (sums, rest, qkv, *_), (gains, shifts, bias, qkv_out, proj, up, down, *_) in zip(ins, outs):
         group = lax.axis_index(FSDP)
         rows = take_own(group, sums[0:8])
         gains[...] = rows[0:2]
@@ -1235,11 +1320,14 @@
         else:
             proj[...] = rest[:, :own].astype(F32)
             down[...] = rest[:, own + hidden :].astype(F32)
+    for _, write in passes:
+        write.wait()
 
 
 def finish(streams):
-    out_shape = []
-    for sums, rest, qkv, flip in streams:
+    vmem, hbm = pl.BlockSpec(memory_space=pltpu.VMEM), pl.BlockSpec(memory_space=pl.ANY)
+    out_shape, scratch = [], []
+    for sums, rest, qkv, y, grad, flip in streams:
         rows, own = qkv.shape[0], qkv.shape[1] // 3
         hidden = (rest.shape[1] - own) // 2
         shapes = [(2, rows), (4, rows), (1, 3 * rows), (3, rows, own)]
@@ -1247,10 +1335,17 @@
             (rows, own), (rows, hidden), (rows, hidden)
         ]
         out_shape += [jax.ShapeDtypeStruct(shape, F32) for shape in shapes]
-    results = pl.pallas_call(finish_kernel, out_shape=out_shape, name="finish")(
-        *streams[0][:3], *streams[1][:3]
-    )
-    return results[:7], results[7:]
+        out_shape += [jax.ShapeDtypeStruct(a.shape, a.dtype) for a in (y, grad)]
+        scratch += [pltpu.VMEM(a.shape, a.dtype) for a in (y, grad)]
+    results = pl.pallas_call(
+        finish_kernel,
+        out_shape=out_shape,
+        in_specs=([vmem] * 3 + [hbm] * 2) * 2,
+        out_specs=([vmem] * 7 + [hbm] * 2) * 2,
+        scratch_shapes=scratch + [pltpu.SemaphoreType.DMA((4,)), pltpu.SemaphoreType.DMA((4,))],
+        name="finish",
+    )(*streams[0][:5], *streams[1][:5])
+    return results[:9], results[9:]
 
 
 def on_device(*args):
@@ -1274,11 +1369,14 @@
             for s, (y, dmid, do, rest, sums) in zip(streams, done)
         ]
     )
-    final = finish([(sums, rest, qkv, s.flip) for s, (_, sums, rest, qkv) in zip(streams, ended)])
+    final = finish(
+        [
+            (sums, rest, qkv, y, grad, s.flip)
+            for s, (y, *_), (grad, sums, rest, qkv) in zip(streams, done, ended)
+        ]
+    )
     outputs = []
-    for s, (y, *_), (grad_rows, *_), (gains, shifts, bias, qkv, proj, up, down) in zip(
-        streams, done, ended, final
-    ):
+    for s, (gains, shifts, bias, qkv, proj, up, down, y, grad_rows) in zip(streams, final):
         if not s.flip:
             proj, down = proj.T, down.T
         outputs.append((y[None], grad_rows[None], gains, shifts, bias, qkv, proj, up, down))

time: 284 us -> 280 us (0.986)
  local copies, waits for them, and re-layouts: 4.03 us -> 0 us
    pallas_call x1, Pallas kernels: 97.3 us -> 86.9 us  [front(): pl.pallas_call(front_kernel, out_shape=out_shape, in_specs=[hbm, vmem, vm...]
    pallas_call x1, Pallas kernels: 137 us -> 143 us  [last(): pl.pallas_call(last_kernel, out_shape=out_shape, in_specs=specs, out_spec...]
    unnamed x12 -> x0, local copies, waits for them, and re-layouts: 4.03 us -> none
    pallas_call x1, Pallas kernels: 4.35 us -> 7.57 us  [finish(): pl.pallas_call(finish_kernel, out_shape=out_shape, in_specs=([vmem] * 3 +...]
where the time goes in v2:
time: 280 us; the launch traced here: 279 us
  Pallas kernels  278 us (99%)
    pallas_call x1, Pallas kernels, last(): pl.pallas_call(last_kernel, out_shape=out_shape, in_specs=specs, out_spec...  143 us
    pallas_call x1, Pallas kernels, front(): pl.pallas_call(front_kernel, out_shape=out_shape, in_specs=[hbm, vmem, vm...  86.9 us
    pallas_call x1, Pallas kernels, middle(): pl.pallas_call(middle_kernel, out_shape=out_shape, in_specs=([hbm] * 3 +...  40.7 us
    pallas_call x1, Pallas kernels, finish(): pl.pallas_call(finish_kernel, out_shape=out_shape, in_specs=([vmem] * 3 +...  7.57 us

profile of v2, /device:TPU:0, one launch (start us, length us, event | category | flops | bytes accessed | tf_op | source)
XLA Modules:
  0.0 279.3 jit_solution(16043793851180743926)
XLA Ops:
  0.7 86.9 %front.1 = (bf16[3,512,256]{2,1,0:T(8,128)(2,1)}, f32[16,512]{1,0:T(8,128)}, bf16[512,512]{1,0:T(8,128)(2,1)}, bf16[4,768,128]{2,1,0:T(8,128)(2,1)}, bf16[512,25...) custom-call(bf16[512,512]{1,0:T(8,128)(2,1)} %bitcast.15, ...), custom_call_target="tpu_custom_call" | custom-call | tf_op jit(solution)/shard_map/front/pallas_call | solution.py:516
  87.5 40.7 %middle.1 = (bf16[512,512]{1,0:T(8,128)(2,1)}, f32[512,512]{1,0:T(8,128)}, bf16[4,256,128]{2,1,0:T(8,128)(2,1)}, f32[128,2304]{1,0:T(8,128)}, f32[16,512]{1,0:T(...) custom-call(bf16[4,256,128]{2,1,0:T(8,128)(2,1)} %get-tuple-element., ...), custom_call_target="tpu_custom_call" | custom-call | tf_op jit(solution)/shard_map/middle/pallas_call | solution.py:977
  128.2 143.3 %last.1 = (f32[512,512]{1,0:T(8,128)}, f32[16,512]{1,0:T(8,128)}, bf16[128,2304]{1,0:T(8,128)(2,1)}, bf16[128,768]{1,0:T(8,128)(2,1)}, f32[512,768]{1,0:T(8,128)...) custom-call(bf16[4,768,128]{2,1,0:T(8,128)(2,1)} %get-tuple-element.74.refs_0_, ...), custom_call_target="tpu_custom_call" | custom-call | tf_op jit(solution)/shard_map/last/pallas_call | solution.py:1270
  271.5 7.6 %finish.1 = (f32[2,128]{1,0:T(2,128)}, f32[4,128]{1,0:T(4,128)}, f32[1,384]{1,0:T(1,128)}, f32[3,128,256]{2,1,0:T(8,128)}, f32[256,128]{1,0:T(8,128)}, /*index=5...) custom-call(f32[16,512]{1,0:T(8,128)} %get-tuple-element.102.refs_0_, ...), custom_call_target="tpu_custom_call" | custom-call | tf_op jit(solution)/shard_map/finish/pallas_call | solution.py:1340

commit v3 on v2

--- a/solution.py
+++ b/solution.py
@@ -1090,20 +1090,28 @@
             key_gradients(image.acc, image.back, 1)
             for copy in shared_sends:
                 copy.start()
-            unattend_tasks(text, text_task, 0, 8, 4, True)
-            key_gradients(text.acc, text.back, 0)
-            for copy in text.sends:
-                copy.start()
-
-        @pl.when(phase == 1)
-        def _():
-            plane.cross()
 
         return carry
 
     lax.fori_loop(0, 3, image_phase, 0)
     key_gradients(image.acc, image.back, 0)
     for copy in own_sends:
+        copy.start()
+
+    text_line.join()
+
+    def text_phase(phase, carry):
+        unattend_tasks(text, text_task, phase * 4, phase * 4 + 4, 4, True)
+
+        @pl.when(phase == 0)
+        def _():
+            plane.cross()
+
+        return carry
+
+    lax.fori_loop(0, 2, text_phase, 0)
+    key_gradients(text.acc, text.back, 0)
+    for copy in text.sends:
         copy.start()
 
     def project(s):
@@ -1171,39 +1179,29 @@
         for begin, end in zip(cuts, cuts[1:])
     ]
 
-    def by_core(one, two):
-        @pl.when(at.core == 0)
-        def _():
-            one()
-            two()
-
-        @pl.when(at.core == 1)
-        def _():
-            two()
-            one()
-
-    project(text)
+    project(image)
     plane.arrived()
-    text.qkv_plane.cross()
-    input_grad(text)
     for line in rest_lines:
         line.gather()
-    text.qkv_plane.arrived()
-    text.qkv_sums[0].gather()
-    add_sums(text, 0)
-    project(image)
-    by_core(rest_lines[0].join, text_line.join)
     input_grad(image)
+    image.qkv_plane.cross()
+    text_line.share()
+    add_sums(image, 0)
+    rest_lines[0].join()
     rest_lines[1].join()
-    image.qkv_plane.cross()
-    add_sums(text, 1)
-    add_sums(image, 0)
-    by_core(rest_lines[0].share, text_line.share)
+    project(text)
     rest_lines[2].join()
+    input_grad(text)
     image.qkv_plane.arrived()
     for line in image.qkv_sums:
         line.gather()
+    text.qkv_plane.cross()
     add_sums(image, 1)
+    add_sums(text, 0)
+    rest_lines[0].share()
+    text.qkv_plane.arrived()
+    text.qkv_sums[0].gather()
+    add_sums(text, 1)
     rest_lines[1].share()
     rest_lines[3].join()
     image.qkv_sums[0].join()
@@ -1286,46 +1284,71 @@
     return pltpu.roll(row, (4 - group) % 4 * columns, 1)[:, :columns]
 
 
+FINISH_IN, FINISH_OUT = 5, 9
+
+
 def finish_kernel(*refs):
-    ins = [refs[:5], refs[5:10]]
-    outs = [refs[10:19], refs[19:28]]
-    buffers, reads, writes = [refs[28:30], refs[30:32]], refs[32], refs[33]
-    passes = []
-    for index, (in_refs, out_refs, own) in enumerate(zip(ins, outs, buffers)):
-        for place in range(2):
-            step = 2 * index + place
-            copy = pltpu.make_async_copy(in_refs[3 + place], own[place], reads.at[step])
+    ins = [refs[:FINISH_IN], refs[FINISH_IN : 2 * FINISH_IN]]
+    refs = refs[2 * FINISH_IN :]
+    outs = [refs[:FINISH_OUT], refs[FINISH_OUT : 2 * FINISH_OUT]]
+    refs = refs[2 * FINISH_OUT :]
+    count = FINISH_IN + FINISH_OUT - 2
+    scratch = [refs[:count], refs[count : 2 * count]]
+    reads, writes = refs[2 * count :]
+    streams, written = [], []
+
+    def write(src, dst):
+        copy = pltpu.make_async_copy(src, dst, writes.at[len(written)])
+        copy.start()
+        written.append(copy)
+
+    for which, (in_refs, own) in enumerate(zip(ins, scratch)):
+        streams.append([])
+        for index in range(FINISH_IN):
+            copy = pltpu.make_async_copy(
+                in_refs[index], own[index], reads.at[which * FINISH_IN + index]
+            )
             copy.start()
-            passes.append(
-                (copy, pltpu.make_async_copy(own[place], out_refs[7 + place], writes.at[step]))
-            )
-    for copy, write in passes:
-        copy.wait()
-        write.start()
-    for (sums, rest, qkv, *_), (gains, shifts, bias, qkv_out, proj, up, down, *_) in zip(ins, outs):
+            streams[which].append(copy)
+    for copies, out, own in reversed(list(zip(streams, outs, scratch))):
+        sums, rest, qkv, y, grad, gains, shifts, bias, qkv_out, proj, up, down = own
+        copies[1].wait()
+        width = qkv.shape[1] // 3
+        hidden = up.shape[1]
+        up[...] = rest[:, width : width + hidden].astype(F32)
+        write(up, out[5])
+        if down.shape[0] > down.shape[1]:
+            down[...] = jnp.transpose(rest[:, width + hidden :].astype(F32))
+            proj[...] = jnp.transpose(rest[:, :width].astype(F32))
+        else:
+            down[...] = rest[:, width + hidden :].astype(F32)
+            proj[...] = rest[:, :width].astype(F32)
+        write(down, out[6])
+        write(proj, out[4])
+        copies[2].wait()
+        for index in range(3):
+            qkv_out[index] = qkv[:, index * width : (index + 1) * width].astype(F32)
+        write(qkv_out, out[3])
+        copies[3].wait()
+        write(y, out[7])
+        copies[4].wait()
+        write(grad, out[8])
+        copies[0].wait()
         group = lax.axis_index(FSDP)
         rows = take_own(group, sums[0:8])
         gains[...] = rows[0:2]
         shifts[...] = rows[2:6]
         line = jnp.concatenate([sums[6:7], sums[7:8], sums[8:9]], axis=1)
         bias[...] = take_own(group, jnp.broadcast_to(line, (8, line.shape[1])))[0:1]
-        own = qkv.shape[1] // 3
-        for which in range(3):
-            qkv_out[which] = qkv[:, which * own : (which + 1) * own].astype(F32)
-        hidden = up.shape[1]
-        up[...] = rest[:, own : own + hidden].astype(F32)
-        if down.shape[0] > down.shape[1]:
-            proj[...] = jnp.transpose(rest[:, :own].astype(F32))
-            down[...] = jnp.transpose(rest[:, own + hidden :].astype(F32))
-        else:
-            proj[...] = rest[:, :own].astype(F32)
-            down[...] = rest[:, own + hidden :].astype(F32)
-    for _, write in passes:
-        write.wait()
+        write(gains, out[0])
+        write(shifts, out[1])
+        write(bias, out[2])
+    for copy in written:
+        copy.wait()
 
 
 def finish(streams):
-    vmem, hbm = pl.BlockSpec(memory_space=pltpu.VMEM), pl.BlockSpec(memory_space=pl.ANY)
+    hbm = pl.BlockSpec(memory_space=pl.ANY)
     out_shape, scratch = [], []
     for sums, rest, qkv, y, grad, flip in streams:
         rows, own = qkv.shape[0], qkv.shape[1] // 3
@@ -1336,16 +1359,22 @@
         ]
         out_shape += [jax.ShapeDtypeStruct(shape, F32) for shape in shapes]
         out_shape += [jax.ShapeDtypeStruct(a.shape, a.dtype) for a in (y, grad)]
-        scratch += [pltpu.VMEM(a.shape, a.dtype) for a in (y, grad)]
+        scratch += [pltpu.VMEM(a.shape, a.dtype) for a in (sums, rest, qkv, y, grad)]
+        scratch += [pltpu.VMEM(shape, F32) for shape in shapes]
     results = pl.pallas_call(
         finish_kernel,
         out_shape=out_shape,
-        in_specs=([vmem] * 3 + [hbm] * 2) * 2,
-        out_specs=([vmem] * 7 + [hbm] * 2) * 2,
-        scratch_shapes=scratch + [pltpu.SemaphoreType.DMA((4,)), pltpu.SemaphoreType.DMA((4,))],
+        in_specs=[hbm] * (2 * FINISH_IN),
+        out_specs=[hbm] * (2 * FINISH_OUT),
+        scratch_shapes=scratch
+        + [
+            pltpu.SemaphoreType.DMA((2 * FINISH_IN,)),
+            pltpu.SemaphoreType.DMA((2 * FINISH_OUT,)),
+        ],
+        compiler_params=pltpu.CompilerParams(vmem_limit_bytes=64 * 1024 * 1000),
         name="finish",
-    )(*streams[0][:5], *streams[1][:5])
-    return results[:9], results[9:]
+    )(*streams[0][:FINISH_IN], *streams[1][:FINISH_IN])
+    return results[:FINISH_OUT], results[FINISH_OUT:]
 
 
 def on_device(*args):

time: 280 us -> 271 us (0.968)
  Pallas kernels: 278 us -> 270 us
    pallas_call x1, Pallas kernels: 143 us -> 137 us  [last(): pl.pallas_call(last_kernel, out_shape=out_shape, in_specs=specs, out_spec...]
where the time goes in v3:
time: 271 us
  Pallas kernels  270 us (100%)
    pallas_call x1, Pallas kernels, last(): pl.pallas_call(last_kernel, out_shape=out_shape, in_specs=specs, out_spec...  137 us
    pallas_call x1, Pallas kernels, front(): pl.pallas_call(front_kernel, out_shape=out_shape, in_specs=[hbm, vmem, vm...  86.9 us
    pallas_call x1, Pallas kernels, middle(): pl.pallas_call(middle_kernel, out_shape=out_shape, in_specs=([hbm] * 3 +...  40.7 us
    pallas_call x1, Pallas kernels, finish(): pl.pallas_call(finish_kernel, out_shape=out_shape, in_specs=[hbm] * (2 *...  5.92 us

profile of v3, /device:TPU:0, one launch (start us, length us, event | category | flops | bytes accessed | tf_op | source)
XLA Modules:
  0.0 270.8 jit_solution(16115230442478373126)
XLA Ops:
  0.7 86.9 %front.1 = (bf16[3,512,256]{2,1,0:T(8,128)(2,1)}, f32[16,512]{1,0:T(8,128)}, bf16[512,512]{1,0:T(8,128)(2,1)}, bf16[4,768,128]{2,1,0:T(8,128)(2,1)}, bf16[512,25...) custom-call(bf16[512,512]{1,0:T(8,128)(2,1)} %bitcast.15, ...), custom_call_target="tpu_custom_call" | custom-call | tf_op jit(solution)/shard_map/front/pallas_call | solution.py:516
  87.5 40.7 %middle.1 = (bf16[512,512]{1,0:T(8,128)(2,1)}, f32[512,512]{1,0:T(8,128)}, bf16[4,256,128]{2,1,0:T(8,128)(2,1)}, f32[128,2304]{1,0:T(8,128)}, f32[16,512]{1,0:T(...) custom-call(bf16[4,256,128]{2,1,0:T(8,128)(2,1)} %get-tuple-element., ...), custom_call_target="tpu_custom_call" | custom-call | tf_op jit(solution)/shard_map/middle/pallas_call | solution.py:977
  128.2 136.5 %last.1 = (f32[512,512]{1,0:T(8,128)}, f32[16,512]{1,0:T(8,128)}, bf16[128,2304]{1,0:T(8,128)(2,1)}, bf16[128,768]{1,0:T(8,128)(2,1)}, f32[512,768]{1,0:T(8,128)...) custom-call(bf16[4,768,128]{2,1,0:T(8,128)(2,1)} %get-tuple-element.74.refs_0_, ...), custom_call_target="tpu_custom_call" | custom-call | tf_op jit(solution)/shard_map/last/pallas_call | solution.py:1268
  264.7 5.9 %finish.1 = (f32[2,128]{1,0:T(2,128)}, f32[4,128]{1,0:T(4,128)}, f32[1,384]{1,0:T(1,128)}, f32[3,128,256]{2,1,0:T(8,128)}, f32[256,128]{1,0:T(8,128)}, /*index=5...) custom-call(f32[16,512]{1,0:T(8,128)} %get-tuple-element.102.refs_0_, ...), custom_call_target="tpu_custom_call" | custom-call | tf_op jit(solution)/shard_map/finish/pallas_call | solution.py:1364

commit v4 on v3

--- a/solution.py
+++ b/solution.py
@@ -314,12 +314,16 @@
     return (4, (heads // 2 - 1) * QB, LANES)
 
 
-def first_rows(x_ref, small_ref, weight_ref, first_ref, qkv_ref, step):
-    width = weight_ref.shape[2]
-    rows = slice(step * 256, step * 256 + 256)
+def first_rows(x_ref, small_ref, normal_ref, first_ref, rows):
     normed, _ = normalise(x_ref[rows, :].astype(F32))
     first = (normed * small_ref[0:1] + small_ref[2:3]).astype(BF16)
+    normal_ref[rows, :] = first
     first_ref[:, rows] = jnp.transpose(first)
+
+
+def project_rows(normal_ref, small_ref, weight_ref, qkv_ref, rows):
+    width = weight_ref.shape[2]
+    first = normal_ref[rows, :]
     bias = small_ref[6:7]
     qkv_ref[rows, :width] = (dot(first, weight_ref[0]) + bias[:, :width]) * 0.125
     qkv_ref[rows, width : 2 * width] = dot(first, weight_ref[1])
@@ -341,7 +345,7 @@
         out[6 + row : 7 + row] = line[0:1, row * width : (row + 1) * width]
 
 
-FRONT_IN, FRONT_OUT, FRONT_SCRATCH = 9, 10, 20
+FRONT_IN, FRONT_OUT, FRONT_SCRATCH = 9, 10, 21
 
 
 def front_kernel(*refs):
@@ -366,7 +370,7 @@
             s.small_in, s.small_own, s.wide, s.flat, s.rows, s.mine, s.got, s.down_t, s.proj_t,
             s.query_doc, s.key_doc, s.score_keys, s.value_keys, s.x, s.up, s.down, s.proj, s.weight, s.first,
         ) = own[:19]
-        s.o = own[19]
+        s.o, s.normal = own[19:]
         s.heads = s.weight.shape[2] // HD
         s.features = (s.query_doc, s.key_doc)
         s.reads = [
@@ -398,9 +402,11 @@
         for copy in s.small_done:
             copy.wait_recv()
         s.small[...] = s.small_own[...] + s.small_in[0] + s.small_in[1] + s.small_in[2]
+        for rows in chunks(s.x.shape[0]):
+            first_rows(s.x, s.small, s.normal, s.first, rows)
         s.gather.arrived()
-        for step in range(s.x.shape[0] // 256):
-            first_rows(s.x, s.small, s.weight, s.first, s.rows, step)
+        for rows in chunks(s.x.shape[0]):
+            project_rows(s.normal, s.small, s.weight, s.rows, rows)
         write_messages(s.rows, s.mine, s.heads)
         s.writes = [copies.local(s.weight, s.weight_out), copies.local(s.first, s.first_out)]
 
@@ -512,6 +518,7 @@
             pltpu.VMEM((3, width, own), BF16),
             pltpu.VMEM((width, tokens), BF16),
             pltpu.VMEM(mixed_shape(own // HD), BF16),
+            pltpu.VMEM((tokens, width), BF16),
         ]
     results = pl.pallas_call(
         front_kernel,
@@ -907,8 +914,8 @@
     proj_grad(text)
     plane = PlaneSum(copies, at, text.rest, arrivals)
     feed_forward(image)
+    plane.cross()
     back(image)
-    plane.cross()
     proj_grad(image)
     keep = copies.local(image.rest, image.rest_out)
     output(text)

time: 271 us -> 269 us (level)
  no operation moved by 1% of the time
where the time goes in v4:
time: 269 us; the launch traced here: 268 us
  Pallas kernels  268 us (100%)
    pallas_call x1, Pallas kernels, last(): pl.pallas_call(last_kernel, out_shape=out_shape, in_specs=specs, out_spec...  134 us
    pallas_call x1, Pallas kernels, front(): pl.pallas_call(front_kernel, out_shape=out_shape, in_specs=[hbm, vmem, vm...  86.6 us
    pallas_call x1, Pallas kernels, middle(): pl.pallas_call(middle_kernel, out_shape=out_shape, in_specs=([hbm] * 3 +...  40.7 us
    pallas_call x1, Pallas kernels, finish(): pl.pallas_call(finish_kernel, out_shape=out_shape, in_specs=[hbm] * (2 *...  5.92 us

profile of v4, /device:TPU:0, one launch (start us, length us, event | category | flops | bytes accessed | tf_op | source)
XLA Modules:
  0.0 268.4 jit_solution(5703381824989340317)
XLA Ops:
  0.7 86.6 %front.1 = (bf16[3,512,256]{2,1,0:T(8,128)(2,1)}, f32[16,512]{1,0:T(8,128)}, bf16[512,512]{1,0:T(8,128)(2,1)}, bf16[4,768,128]{2,1,0:T(8,128)(2,1)}, bf16[512,25...) custom-call(bf16[512,512]{1,0:T(8,128)(2,1)} %bitcast.15, ...), custom_call_target="tpu_custom_call" | custom-call | tf_op jit(solution)/shard_map/front/pallas_call | solution.py:523
  87.3 40.7 %middle.1 = (bf16[512,512]{1,0:T(8,128)(2,1)}, f32[512,512]{1,0:T(8,128)}, bf16[4,256,128]{2,1,0:T(8,128)(2,1)}, f32[128,2304]{1,0:T(8,128)}, f32[16,512]{1,0:T(...) custom-call(bf16[4,256,128]{2,1,0:T(8,128)(2,1)} %get-tuple-element., ...), custom_call_target="tpu_custom_call" | custom-call | tf_op jit(solution)/shard_map/middle/pallas_call | solution.py:984
  128.0 134.3 %last.1 = (f32[512,512]{1,0:T(8,128)}, f32[16,512]{1,0:T(8,128)}, bf16[128,2304]{1,0:T(8,128)(2,1)}, bf16[128,768]{1,0:T(8,128)(2,1)}, f32[512,768]{1,0:T(8,128)...) custom-call(bf16[4,768,128]{2,1,0:T(8,128)(2,1)} %get-tuple-element.74.refs_0_, ...), custom_call_target="tpu_custom_call" | custom-call | tf_op jit(solution)/shard_map/last/pallas_call | solution.py:1275
  262.3 5.9 %finish.1 = (f32[2,128]{1,0:T(2,128)}, f32[4,128]{1,0:T(4,128)}, f32[1,384]{1,0:T(1,128)}, f32[3,128,256]{2,1,0:T(8,128)}, f32[256,128]{1,0:T(8,128)}, /*index=5...) custom-call(f32[16,512]{1,0:T(8,128)} %get-tuple-element.102.refs_0_, ...), custom_call_target="tpu_custom_call" | custom-call | tf_op jit(solution)/shard_map/finish/pallas_call | solution.py:1371

commit v5 on v4

--- a/solution.py
+++ b/solution.py
@@ -765,7 +765,8 @@
     refs = refs[2 * MIDDLE_OUT :]
     scratch = [refs[:MIDDLE_SCRATCH], refs[MIDDLE_SCRATCH : 2 * MIDDLE_SCRATCH]]
     arrivals = refs[2 * MIDDLE_SCRATCH : 2 * MIDDLE_SCRATCH + 4]
-    copies = Copies(*refs[2 * MIDDLE_SCRATCH + 4 :])
+    near = refs[2 * MIDDLE_SCRATCH + 4]
+    copies = Copies(*refs[2 * MIDDLE_SCRATCH + 5 :])
     others = [at.to_x, at.to_y] + at.to_ctx[1:] + [at.to_core]
     greet(others)
     streams = []
@@ -786,14 +787,14 @@
     text, image = streams
     text.rest_done = [copies.local(src, dst) for src, dst in text.weights]
     quarter = image.up.shape[0] // 4
-    near = [
+    close = [
         pl.ds(pl.multiple_of(owner * quarter, 8), quarter)
         for owner in (at.group, at.group_x, at.group_y)
     ]
     image.rest_done = [
         copies.local(src.at[rows, :], dst.at[rows, :])
         for src, dst in image.weights
-        for rows in near
+        for rows in close
     ]
     meet(others)
     top = pl.ds(pl.multiple_of(at.group_y * quarter, 8), quarter // 2)
@@ -924,11 +925,13 @@
     half = plane.half
 
     def put(cols):
-        text.rest_out[:half, cols], text.rest_out[half:, cols] = plane.halves(cols)
+        near[:half, cols], near[half:, cols] = plane.halves(cols)
 
     by_columns(plane.columns, put)
+    near_done = copies.local(near, text.rest_out)
     plane.sent()
     keep.wait()
+    near_done.wait()
     for s in streams:
         for copy in s.do_done + s.writes:
             copy.wait()
@@ -947,6 +950,7 @@
         summed = arrivals is None
         if summed:
             arrivals = PlaneSum.arrivals(width // 4, rest[1])
+            arrivals.append(pltpu.VMEM((width // 4, rest[1]), F32))
         out_shape += [
             jax.ShapeDtypeStruct((tokens, width), BF16),
             jax.ShapeDtypeStruct((tokens, width), F32),
@@ -956,7 +960,7 @@
             else jax.ShapeDtypeStruct(rest, BF16),
             jax.ShapeDtypeStruct(small.shape, F32),
         ]
-        out_specs += [hbm, hbm, hbm, vmem if summed else hbm, vmem]
+        out_specs += [hbm, hbm, hbm, hbm, vmem]
         scratch += [
             pltpu.VMEM(proj.shape, BF16),
             pltpu.VMEM(up.shape, BF16),
@@ -986,7 +990,7 @@
         out_shape=out_shape,
         in_specs=([hbm] * 3 + [vmem] + [hbm] * 3) * 2,
         out_specs=out_specs,
-        scratch_shapes=scratch + arrivals + copy_sems(2 * 6 + 4 + 6, 2 * (4 + 3) + 8 + 1),
+        scratch_shapes=scratch + arrivals + copy_sems(2 * 6 + 4 + 6, 2 * (4 + 3) + 8 + 2),
         compiler_params=pltpu.CompilerParams(
             collective_id=1, has_side_effects=True, vmem_limit_bytes=64 * 1024 * 1000
         ),
@@ -1027,8 +1031,8 @@
     count = LAST_SCRATCH + 10
     scratch = [refs[:count], refs[count : 2 * count]]
     refs = refs[2 * count :]
-    rest_arrivals, rest_loads = refs[:4], refs[4:7]
-    copies = Copies(*refs[7:])
+    rest_arrivals, rest_loads, text_near = refs[:4], refs[4:7], refs[7]
+    copies = Copies(*refs[8:])
     others = [at.to_x, at.to_y] + at.to_ctx[1:] + [at.to_core]
     greet(others)
     streams = []
@@ -1052,20 +1056,25 @@
         ]
         streams.append(s)
     text, image = streams
-    for s in streams:
+
+    def prepare(s):
         document_features(s.seg_row, *s.features)
         s.acc[...] = jnp.zeros_like(s.acc)
         s.back[...] = jnp.zeros_like(s.back)
+
+    rest_done = copies.local(text.rest, text_near)
+    prepare(image)
     meet(others)
     plane = PlaneSum(copies, at, image.rest, rest_arrivals, rest_loads)
-    text_half = text.rest.shape[0] // 2
+    text_half = text_near.shape[0] // 2
 
     def text_values(cols):
-        return text.rest[:text_half, cols], text.rest[text_half:, cols]
+        return text_near[:text_half, cols], text_near[text_half:, cols]
 
     text_line = LineSum(
         copies, at, text_values, text.rest_line, text.rest_final, 0, text.rest.shape[1]
     )
+    rest_done.wait()
     text_line.gather()
     for s in (image, text):
         for copy in s.reads:
@@ -1076,7 +1085,7 @@
                 (s.first_in, s.first), (s.weight_in, s.weight), (s.x_in, s.x), (s.dmid_in, s.dmid),
             )
         ]
-        mark_keys(s.m, s.features[1], s.acc.shape[0], s.score_keys, None)
+    mark_keys(image.m, image.features[1], 2, image.score_keys, None)
 
     def unattend_tasks(s, *task):
         unattend(
@@ -1106,6 +1115,8 @@
         copy.start()
 
     text_line.join()
+    prepare(text)
+    mark_keys(text.m, text.features[1], 1, text.score_keys, None)
 
     def text_phase(phase, carry):
         unattend_tasks(text, text_task, phase * 4, phase * 4 + 4, 4, True)
@@ -1270,14 +1281,15 @@
         scratch += LineSum.scratch(*rest_shape) + LineSum.scratch(*qkv_shape)
         scratch += PlaneSum.arrivals(*qkv_shape)
     scratch += PlaneSum.arrivals(*rest_shape) + PlaneSum.loads_scratch(*rest_shape)
-    specs = [hbm, hbm, hbm, vmem, vmem, hbm, hbm, vmem, hbm, hbm, vmem, vmem]
+    scratch += [pltpu.VMEM(streams[0][10].shape, F32)]
+    specs = [hbm, hbm, hbm, vmem, vmem, hbm, hbm, vmem, hbm, hbm, hbm, vmem]
     specs += specs[:10] + [hbm, vmem]
     results = pl.pallas_call(
         last_kernel,
         out_shape=out_shape,
         in_specs=specs,
         out_specs=[hbm, vmem, vmem, vmem] * 2,
-        scratch_shapes=scratch + copy_sems(2 * (3 + 1 + 5 + 6) + 3 + 6 + 3 * 8, 2 * (1 + 7 + 1) + 3 + 1),
+        scratch_shapes=scratch + copy_sems(2 * (3 + 1 + 5 + 6) + 3 + 6 + 3 * 8, 2 * (1 + 7 + 1) + 3 + 2),
         compiler_params=pltpu.CompilerParams(
             collective_id=2, has_side_effects=True, vmem_limit_bytes=64 * 1024 * 1000
         ),

time: 269 us -> 269 us (level)
  no operation moved by 1% of the time
where the time goes in v5:
time: 269 us; the launch traced here: 268 us
  Pallas kernels  268 us (100%)
    pallas_call x1, Pallas kernels, last(): pl.pallas_call(last_kernel, out_shape=out_shape, in_specs=specs, out_spec...  135 us
    pallas_call x1, Pallas kernels, front(): pl.pallas_call(front_kernel, out_shape=out_shape, in_specs=[hbm, vmem, vm...  86.6 us
    pallas_call x1, Pallas kernels, middle(): pl.pallas_call(middle_kernel, out_shape=out_shape, in_specs=([hbm] * 3 +...  40.3 us
    pallas_call x1, Pallas kernels, finish(): pl.pallas_call(finish_kernel, out_shape=out_shape, in_specs=[hbm] * (2 *...  5.92 us

profile of v5, /device:TPU:0, one launch (start us, length us, event | category | flops | bytes accessed | tf_op | source)
XLA Modules:
  0.0 268.5 jit_solution(17137025415795205092)
XLA Ops:
  0.7 86.6 %front.1 = (bf16[3,512,256]{2,1,0:T(8,128)(2,1)}, f32[16,512]{1,0:T(8,128)}, bf16[512,512]{1,0:T(8,128)(2,1)}, bf16[4,768,128]{2,1,0:T(8,128)(2,1)}, bf16[512,25...) custom-call(bf16[512,512]{1,0:T(8,128)(2,1)} %bitcast.15, ...), custom_call_target="tpu_custom_call" | custom-call | tf_op jit(solution)/shard_map/front/pallas_call | solution.py:523
  87.3 40.3 %middle.1 = (bf16[512,512]{1,0:T(8,128)(2,1)}, f32[512,512]{1,0:T(8,128)}, bf16[4,256,128]{2,1,0:T(8,128)(2,1)}, f32[128,2304]{1,0:T(8,128)}, f32[16,512]{1,0:T(...) custom-call(bf16[4,256,128]{2,1,0:T(8,128)(2,1)} %get-tuple-element., ...), custom_call_target="tpu_custom_call" | custom-call | tf_op jit(solution)/shard_map/middle/pallas_call | solution.py:988
  127.6 134.8 %last.1 = (f32[512,512]{1,0:T(8,128)}, f32[16,512]{1,0:T(8,128)}, bf16[128,2304]{1,0:T(8,128)(2,1)}, bf16[128,768]{1,0:T(8,128)(2,1)}, f32[512,768]{1,0:T(8,128)...) custom-call(bf16[4,768,128]{2,1,0:T(8,128)(2,1)} %get-tuple-element.74.refs_0_, ...), custom_call_target="tpu_custom_call" | custom-call | tf_op jit(solution)/shard_map/last/pallas_call | solution.py:1287
  262.4 5.9 %finish.1 = (f32[2,128]{1,0:T(2,128)}, f32[4,128]{1,0:T(4,128)}, f32[1,384]{1,0:T(1,128)}, f32[3,128,256]{2,1,0:T(8,128)}, f32[256,128]{1,0:T(8,128)}, /*index=5...) custom-call(f32[16,512]{1,0:T(8,128)} %get-tuple-element.102.refs_0_, ...), custom_call_target="tpu_custom_call" | custom-call | tf_op jit(solution)/shard_map/finish/pallas_call | solution.py:1383
